TPU v7x, 32 devices: a whole 2x2x4 slice. The times are simulated.
32 devices in a mesh: runs: 2 (over y), lon: 4 (over x, core), lat: 4 (over z).
Axes of the slice: x: 2, y: 2, z: 4, core: 2. Of those that a mesh axis runs over, the one named last changes fastest.
Arguments:
- latent: bfloat16 [8, 24, 48, 512], P('runs', 'lat', 'lon'), parts along dimension 0, may hold values from -16 to 16
- cotangent: bfloat16 [8, 24, 48, 512], P('runs', 'lat', 'lon'), parts along dimension 0, may hold values from -6 to 6
- mask_ids: int32 [8, 24, 48], P('runs', 'lat', 'lon'), parts along dimension 0, may hold values from 0 to 1
- position_bias: float32 [8, 37], replicated, may hold values from -2 to 302
- norm_gain: float32 [512], replicated, may hold values from 0.1 to 1.9
- w_qkv: bfloat16 [512, 1536], replicated, may hold values from -0.25 to 0.25
- qkv_down: bfloat16 [16, 512], replicated, may hold values from -0.25 to 0.25
- qkv_up: bfloat16 [16, 1536], replicated, may hold values from -0.75 to 0.75
- w_proj: bfloat16 [512, 512], replicated, may hold values from -0.25 to 0.25
- proj_down: bfloat16 [16, 512], replicated, may hold values from -0.25 to 0.25
- proj_up: bfloat16 [16, 512], replicated, may hold values from -0.75 to 0.75
Outputs:
- output: bfloat16 [8, 24, 48, 512], P('runs', 'lat', 'lon'), parts along dimension 0
- latent_grad: bfloat16 [8, 24, 48, 512], P('runs', 'lat', 'lon'), parts along dimension 0
- qkv_down_grad: float32 [32, 512], P('runs'), parts along dimension 0
- qkv_up_grad: float32 [32, 1536], P('runs'), parts along dimension 0
- proj_down_grad: float32 [32, 512], P('runs'), parts along dimension 0
- proj_up_grad: float32 [32, 512], P('runs'), parts along dimension 0
There are 2 independent parts, one for each index of `runs`. A program takes and returns all parts, laid end to end along the dimension named above; an argument that names none is the same for every part. Nothing has to cross between parts.
All inputs are finite; a program needn't handle non-finite values.
Results may differ from a plain program's by a relative error of at most 0.011.
Values may be sent and summed in bfloat16 or wider, within the bound.
A program may use at most 64 MiB of HBM per device.

v0:
```python
import math

import jax
import jax.numpy as jnp
from jax import lax
from jax.sharding import PartitionSpec as P

HEADS = 8
WIN_LEV = 2
WIN_LAT = 6
WIN_LON = 12


epsilon = 1e-05
masked_value = -1e30


def from_behind(array, axis, by):
    length = lax.axis_size(axis)
    return lax.ppermute(array, axis, [(i, (i + by) % length) for i in range(length)])


def dot_rows(left_side, right_side):
    return lax.dot_general(
        left_side, right_side, (((1,), (1,)), ((), ())), preferred_element_type=jnp.float32
    )


def dot_cols(left_side, right_side):
    return lax.dot_general(
        left_side, right_side, (((0,), (0,)), ((), ())), preferred_element_type=jnp.float32
    )


def window_bias(position_bias):
    window_size = WIN_LEV * WIN_LAT * WIN_LON
    places = jnp.arange(window_size, dtype=jnp.int32)
    level_pos = places // (WIN_LAT * WIN_LON)
    lat_pos = places // WIN_LON % WIN_LAT
    lon_pos = places % WIN_LON
    level_col = level_pos[:, None] - level_pos[None, :] + WIN_LEV - 1
    lat_col = lat_pos[:, None] - lat_pos[None, :] + 2 * WIN_LEV - 1 + WIN_LAT - 1
    lon_col = lon_pos[:, None] - lon_pos[None, :] + 2 * WIN_LEV + 2 * WIN_LAT - 2 + WIN_LON - 1
    columns = jnp.arange(position_bias.shape[1], dtype=jnp.int32)[:, None, None]
    one_hot = (columns == level_col[None]) | (columns == lat_col[None]) | (columns == lon_col[None])
    one_hot = one_hot.astype(jnp.float32).reshape(position_bias.shape[1], window_size * window_size)
    table = jnp.dot(position_bias, one_hot, precision=lax.Precision.HIGHEST)
    return table.reshape(position_bias.shape[0], window_size, window_size)


def to_windows(grid):
    levels, lat_rows, lon_cols, chans = grid.shape
    blocks = grid.reshape(
        levels // WIN_LEV,
        WIN_LEV,
        lat_rows // WIN_LAT,
        WIN_LAT,
        lon_cols // WIN_LON,
        WIN_LON,
        chans,
    )
    return blocks.transpose(0, 2, 4, 1, 3, 5, 6).reshape(-1, WIN_LEV * WIN_LAT * WIN_LON, chans)


def from_windows(windows, levels, lat_rows, lon_cols):
    chans = windows.shape[-1]
    blocks = windows.reshape(
        levels // WIN_LEV,
        lat_rows // WIN_LAT,
        lon_cols // WIN_LON,
        WIN_LEV,
        WIN_LAT,
        WIN_LON,
        chans,
    )
    return blocks.transpose(0, 3, 1, 4, 2, 5, 6).reshape(levels, lat_rows, lon_cols, chans)


def attach(kept, received, axis_pos, after):
    joined = []
    start = 0
    for piece in kept:
        chans = piece.shape[3]
        start = start + chans
        if after:
            joined.append(jnp.concatenate((piece, received), axis_pos))
        else:
            joined.append(jnp.concatenate((received, piece), axis_pos))
    return joined


def lon_in(pieces):
    half_cols = WIN_LON // 2
    strip = jnp.concatenate([piece[:, :, :half_cols] for piece in pieces], 3)
    received = from_behind(strip, "lon", -1)
    return attach([piece[:, :, half_cols:] for piece in pieces], received, 2, True)


def lat_in(pieces):
    half_rows = WIN_LAT // 2
    strip = jnp.concatenate([piece[:, :half_rows] for piece in pieces], 3)
    received = from_behind(strip, "lat", -1)
    return attach([piece[:, half_rows:] for piece in pieces], received, 1, True)


def lon_out(pieces):
    half_cols = WIN_LON // 2
    strip = jnp.concatenate([piece[:, :, -half_cols:] for piece in pieces], 3)
    received = from_behind(strip, "lon", 1)
    return attach([piece[:, :, :-half_cols] for piece in pieces], received, 2, False)


def lat_out(pieces):
    half_rows = WIN_LAT // 2
    strip = jnp.concatenate([piece[:, -half_rows:] for piece in pieces], 3)
    received = from_behind(strip, "lat", 1)
    return attach([piece[:, :-half_rows] for piece in pieces], received, 1, False)


def roll_in(pieces):
    pieces = lat_in(lon_in(pieces))
    return [jnp.roll(piece, -(WIN_LEV // 2), axis=0) for piece in pieces]


def roll_out(pieces):
    pieces = [jnp.roll(piece, WIN_LEV // 2, axis=0) for piece in pieces]
    return lat_out(lon_out(pieces))


def forward_pass(
    x_windows,
    id_windows,
    bias_table,
    norm_gain,
    w_qkv,
    qkv_down,
    qkv_up,
    w_proj,
    proj_down,
    proj_up,
):
    windows, window_size, width = x_windows.shape
    rows_total = windows * window_size
    head_size = width // HEADS
    score_scale = 1.0 / math.sqrt(head_size)
    flat_rows = x_windows.reshape(rows_total, width).astype(jnp.float32)
    average = jnp.mean(flat_rows, axis=-1, keepdims=True)
    centered = flat_rows - average
    variance = jnp.mean(centered * centered, axis=-1, keepdims=True)
    inv_std = lax.rsqrt(variance + epsilon)
    unit_rows = centered * inv_std
    normed = (unit_rows * norm_gain).astype(jnp.bfloat16)
    low_qkv = dot_rows(normed, qkv_down).astype(jnp.bfloat16)
    qkv = (
        jnp.dot(normed, w_qkv, preferred_element_type=jnp.float32)
        + jnp.dot(low_qkv, qkv_up, preferred_element_type=jnp.float32)
    ).astype(jnp.bfloat16)
    pieces = qkv.reshape(windows, window_size, 3, HEADS, head_size)
    query, keys, values = (pieces[:, :, 0], pieces[:, :, 1], pieces[:, :, 2])
    allowed = id_windows[:, None, :, None] == id_windows[:, None, None, :]
    scores = (
        jnp.einsum("bqhd,bkhd->bhqk", query, keys, preferred_element_type=jnp.float32) * score_scale
        + bias_table[None]
    )
    scores = jnp.where(allowed, scores, masked_value)
    row_max = jnp.max(scores, axis=-1, keepdims=True)
    exp_terms = jnp.where(allowed, jnp.exp(scores - row_max), 0.0)
    probs_full = exp_terms / jnp.sum(exp_terms, axis=-1, keepdims=True)
    probs = probs_full.astype(jnp.bfloat16)
    attn = jnp.einsum("bhqk,bkhd->bqhd", probs, values, preferred_element_type=jnp.float32)
    attn = attn.astype(jnp.bfloat16).reshape(rows_total, width)
    low_proj = dot_rows(attn, proj_down).astype(jnp.bfloat16)
    out_rows = (
        flat_rows
        + jnp.dot(attn, w_proj, preferred_element_type=jnp.float32)
        + jnp.dot(low_proj, proj_up, preferred_element_type=jnp.float32)
    ).astype(jnp.bfloat16)
    saved = (
        unit_rows,
        inv_std,
        normed,
        low_qkv,
        query,
        keys,
        values,
        probs_full,
        probs,
        attn,
        low_proj,
    )
    return (out_rows.reshape(x_windows.shape), saved)


def backward_proj(grad_windows, saved, w_proj, proj_down, proj_up):
    attn, low_proj = (saved[9], saved[10])
    grad_rows = grad_windows.reshape(attn.shape)
    proj_up_raw = dot_cols(low_proj, grad_rows)
    d_low_proj = dot_rows(grad_rows, proj_up).astype(jnp.bfloat16)
    proj_down_raw = dot_cols(d_low_proj, attn)
    d_attn = (
        dot_rows(grad_rows, w_proj)
        + jnp.dot(d_low_proj, proj_down, preferred_element_type=jnp.float32)
    ).astype(jnp.bfloat16)
    return (d_attn, proj_down_raw, proj_up_raw)


def backward_qkv(grad_windows, d_attn, saved, norm_gain, w_qkv, qkv_down, qkv_up):
    unit_rows, inv_std, normed, low_qkv, query, keys, values, probs_full, probs = saved[:9]
    windows, window_size, width = grad_windows.shape
    rows_total = windows * window_size
    head_size = width // HEADS
    score_scale = 1.0 / math.sqrt(head_size)
    d_heads = d_attn.reshape(windows, window_size, HEADS, head_size)
    d_probs = jnp.einsum("bqhd,bkhd->bhqk", d_heads, values, preferred_element_type=jnp.float32)
    d_values = jnp.einsum("bhqk,bqhd->bkhd", probs, d_heads, preferred_element_type=jnp.float32)
    d_scores = (
        probs_full * (d_probs - jnp.sum(d_probs * probs_full, axis=-1, keepdims=True)) * score_scale
    ).astype(jnp.bfloat16)
    d_query = jnp.einsum("bhqk,bkhd->bqhd", d_scores, keys, preferred_element_type=jnp.float32)
    d_keys = jnp.einsum("bhqk,bqhd->bkhd", d_scores, query, preferred_element_type=jnp.float32)
    d_qkv = (
        jnp.stack([d_query, d_keys, d_values], axis=2)
        .astype(jnp.bfloat16)
        .reshape(rows_total, 3 * width)
    )
    qkv_up_raw = dot_cols(low_qkv, d_qkv)
    d_low_qkv = dot_rows(d_qkv, qkv_up).astype(jnp.bfloat16)
    qkv_down_raw = dot_cols(d_low_qkv, normed)
    d_normed = dot_rows(d_qkv, w_qkv) + jnp.dot(
        d_low_qkv, qkv_down, preferred_element_type=jnp.float32
    )
    d_unit = d_normed * norm_gain
    norm_back = inv_std * (
        d_unit
        - jnp.mean(d_unit, axis=-1, keepdims=True)
        - unit_rows * jnp.mean(d_unit * unit_rows, axis=-1, keepdims=True)
    )
    grad_rows = grad_windows.reshape(rows_total, width).astype(jnp.float32)
    grad_in = (grad_rows + norm_back).astype(jnp.bfloat16)
    return (grad_in.reshape(grad_windows.shape), qkv_down_raw, qkv_up_raw)


def on_device(
    latent,
    cotangent,
    mask_ids,
    position_bias,
    norm_gain,
    w_qkv,
    qkv_down,
    qkv_up,
    w_proj,
    proj_down,
    proj_up,
):
    levels, lat_rows, lon_cols, width = latent.shape
    shifted = roll_in([latent])[0]
    bias_table = window_bias(position_bias)
    id_windows = to_windows(mask_ids[..., None])[..., 0]
    out_windows, saved = forward_pass(
        to_windows(shifted),
        id_windows,
        bias_table,
        norm_gain,
        w_qkv,
        qkv_down,
        qkv_up,
        w_proj,
        proj_down,
        proj_up,
    )
    shifted_out = from_windows(out_windows, levels, lat_rows, lon_cols)
    output = roll_out([shifted_out])[0]
    grad_shifted = roll_in([cotangent])[0]
    grad_windows = to_windows(grad_shifted)
    d_attn, proj_down_raw, proj_up_raw = backward_proj(
        grad_windows, saved, w_proj, proj_down, proj_up
    )
    proj_down_raw, proj_up_raw = lax.psum((proj_down_raw, proj_up_raw), ("lon", "lat"))
    back_windows, qkv_down_raw, qkv_up_raw = backward_qkv(
        grad_windows, d_attn, saved, norm_gain, w_qkv, qkv_down, qkv_up
    )
    qkv_down_raw, qkv_up_raw = lax.psum((qkv_down_raw, qkv_up_raw), ("lon", "lat"))
    grad_in = from_windows(back_windows, levels, lat_rows, lon_cols)
    latent_grad = roll_out([grad_in])[0]
    grad_scale = 1.0 / math.sqrt(
        levels * lat_rows * lon_cols * lax.axis_size("lat") * lax.axis_size("lon")
    )
    return (
        output,
        latent_grad,
        qkv_down_raw * grad_scale,
        qkv_up_raw * grad_scale,
        proj_down_raw * grad_scale,
        proj_up_raw * grad_scale,
    )


def solution(mesh):
    return jax.shard_map(
        on_device,
        mesh=mesh,
        in_specs=(
            P("runs", "lat", "lon", None),
            P("runs", "lat", "lon", None),
            P("runs", "lat", "lon"),
            P(),
            P(),
            P(),
            P(),
            P(),
            P(),
            P(),
            P(),
        ),
        out_specs=(
            P("runs", "lat", "lon", None),
            P("runs", "lat", "lon", None),
            P("runs", None),
            P("runs", None),
            P("runs", None),
            P("runs", None),
        ),
        check_vma=False,
    )
```

profile of v0, /device:TPU:0, one launch (start us, length us, event | category | flops | bytes accessed | tf_op | source)
XLA Modules:
  0.0 297.6 jit_solution(11945016169374373017)
XLA Ops:
  8.4 2.5 collective-permute-start
  15.6 2.5 convolution_bitcast_fusion
  19.0 3.6 %collective-permute-start.1 = (bf16[4,3,12,512]{3,0,2,1:T(4,128)(2,1)}, bf16[4,3,12,512]{3,0,2,1:T(4,128)(2,1)S(1)}, u32[]{:S(2)}, u32[]{:S(2)}) collective-permute-start(bf16[4,3,12,512]{3,0,2,1:T(4,128)(2,1)} %get-tuple-element.25), channel_id=1, source_target_pairs={{0,3},{1,0},{2,1},{3,2},{4,7},{5,4},{6,5},{7,6},{8,11},{9,8},{10,9... | collective-permute-start | bytes 442376 | tf_op jit(solution)/shard_map/ppermute | solution.py:20
  23.3 2.0 add.150
  25.3 1.6 copy.84
  30.1 3.3 %collective-permute-done.5 = bf16[4,3,12,512]{3,0,2,1:T(4,128)(2,1)} collective-permute-done((bf16[4,3,12,512]{3,0,2,1:T(4,128)(2,1)}, bf16[4,3,12,512]{3,0,2,1:T(4,128)(2,1)}, u32[]{:S(2)}, u32[]{:S(2)}) %collective-permute-start.5) | collective-permute-done | bytes 147488 | tf_op jit(solution)/shard_map/ppermute | solution.py:20
  39.1 2.2 reshape.236
  41.3 2.6 fusion.85
  43.9 2.2 copy.103
  46.1 2.2 copy.102
  49.5 4.3 %fusion.90 = (f32[2,8,144]{2,1,0:T(8,128)S(1)}, f32[2,8,144,144]{2,3,1,0:T(8,128)}) fusion(f32[8,144,144]{1,2,0:T(8,128)} %copy.84, pred[2,144,144]{1,2,0:T(8,128)(4,1)S(1)} %copy-done.14, bf16[2,144,1,8,64]{1,4,3,0,2:T(8,128)(2,1)} %copy.104, bf16[2,144,1,8,64]{1,4,3,0,2:T(8,128)(2,1)} %copy.103), kind=kOutput, calls=%fused_computation.130 | convolution fusion | flops 44458128 | bytes 2631168 | tf_op jit(solution)/shard_map/sub | solution.py:167
  53.9 2.8 fusion.26
  63.7 3.2 %fusion.27 = bf16[2,144,1,8,64]{1,4,3,0,2:T(8,128)(2,1)} fusion(bf16[2,144,8,64]{1,3,2,0:T(8,128)(2,1)} %copy.90, f32[2,8,144,144]{2,3,1,0:T(8,128)} %get-tuple-element.29, f32[2,8,144]{2,1,0:T(8,128)S(1)} %get-tuple-element.28), kind=kOutput, calls=%fused_computation.32 | convolution fusion | flops 43278336 | bytes 1926144 | tf_op jit(solution)/shard_map/bhqk,bqhd->bkhd/dot_general | solution.py:215
  66.9 2.0 fusion.49
  68.9 5.5 %fusion.31 = bf16[2,144,1,8,64]{1,4,3,0,2:T(8,128)(2,1)} fusion(f32[2,8,144,144]{2,3,1,0:T(8,128)} %fusion.49, bf16[2,144,1,8,64]{1,4,3,0,2:T(8,128)(2,1)S(1)} %copy-done.9, f32[2,8,144,144]{2,3,1,0:T(8,128)} %get-tuple-element.29, f32[2,8,144]{2,1,0:T(8,128)} %copy-done.28), kind=kOutput, calls=%fused_computation.34 | convolution fusion | flops 44939664 | bytes 3253248 | tf_op jit(solution)/shard_map/bhqk,bkhd->bqhd/dot_general | solution.py:219
  74.4 5.5 %fusion.28 = bf16[2,144,1,8,64]{1,4,3,0,2:T(8,128)(2,1)} fusion(f32[2,8,144,144]{2,3,1,0:T(8,128)} %fusion.49, bf16[2,144,1,8,64]{1,4,3,0,2:T(8,128)(2,1)S(1)} %copy-done.8, f32[2,8,144,144]{2,3,1,0:T(8,128)} %get-tuple-element.29, f32[2,8,144]{2,1,0:T(8,128)} %copy-done.28), kind=kOutput, calls=%fused_computation.33 | convolution fusion | flops 44939664 | bytes 3253248 | tf_op jit(solution)/shard_map/bhqk,bqhd->bkhd/dot_general | solution.py:220
  79.9 2.7 pad_maximum_fusion
  82.6 3.9 %copy.95 = bf16[2,144,3,8,64]{4,3,2,1,0:T(8,128)(2,1)} copy(bf16[2,144,3,8,64]{1,4,3,0,2:T(8,128)(2,1)} %pad_maximum_fusion) | data formatting | bytes 1769472 | tf_op jit(solution)/shard_map/stack | solution.py:222
  86.5 2.9 convert_element_type.73
  90.6 1.7 fusion.98
  96.2 88.8 %all-reduce.6.cloned.1.call-done = (f32[16,512]{1,0:T(8,128)}, f32[16,512]{1,0:T(8,128)}, f32[16,512]{1,0:T(8,128)}) async-done(((f32[16,512]{1,0:T(8,128)}, f32[16,512]{1,0:T(8,128)}, f32[16,512]{1,0:T(8,128)}), (f32[16,512]{1,0:T(8,128)}, f32[16,512]{1,0:T(8,128)}, f32[16,512]{1,0:T(8,128)})) %all-reduce.6.cloned.1.call-update) | async-done | bytes 98320 | tf_op jit(solution)/shard_map/psum | solution.py:283
  186.4 90.3 %all-reduce.4.cloned.1.call-done = f32[16,1536]{1,0:T(8,128)} async-done(((f32[16,1536]{1,0:T(8,128)}), f32[16,1536]{1,0:T(8,128)}) %all-reduce.4.cloned.1.call-update) | async-done | bytes 98320 | tf_op jit(solution)/shard_map/psum | solution.py:283
  276.8 1.5 broadcast_multiply_fusion
  283.1 5.1 %collective-permute-done.3 = bf16[4,3,12,512]{3,0,2,1:T(4,128)(2,1)S(1)} collective-permute-done((bf16[4,3,12,512]{3,0,2,1:T(4,128)(2,1)S(1)}, bf16[4,3,12,512]{3,0,2,1:T(4,128)(2,1)S(1)}, u32[]{:S(2)}, u32[]{:S(2)}) %collective-permute-start.3) | collective-permute-done | bytes 147488 | tf_op jit(solution)/shard_map/ppermute | solution.py:20
  (160 shorter events, 37.9 us)
Async XLA Ops:
  7.2 30.7 %copy-start = (bf16[512,1536]{1,0:T(8,128)(2,1)S(1)}, bf16[512,1536]{1,0:T(8,128)(2,1)}, u32[]{:S(2)}) copy-start(bf16[512,1536]{1,0:T(8,128)(2,1)} %param.16) | copy-start | bytes 4718596
  7.2 8.4 %copy-start.27 = (f32[8,37]{1,0:T(8,128)S(1)}, f32[8,37]{1,0:T(8,128)}, u32[]{:S(2)}) copy-start(f32[8,37]{1,0:T(8,128)} %param.14) | copy-start | bytes 3556
  7.2 177.9 %all-reduce.6.cloned.1.call-start = ((), (), s32[]{:S(2)}) async-start(), calls=%async_computation.1 | async-start | bytes 196608 | tf_op jit(solution)/shard_map/psum | solution.py:283
  8.4 9.7 %collective-permute-start = (bf16[4,6,6,512]{3,0,2,1:T(4,128)(2,1)S(1)}, bf16[4,6,6,512]{3,0,2,1:T(4,128)(2,1)S(1)}, u32[]{:S(2)}, u32[]{:S(2)}) collective-permute-start(bf16[4,6,6,512]{3,0,2,1:T(4,128)(2,1)S(1)} %get-tuple-element.27), channel_id=1, source_target_pairs={{0,12},{4,0},{8,4},{12,8},{1,13},{5,1},{9,5},{13,9},{2,14},{6,2},{... | collective-permute-start | bytes 442376 | tf_op jit(solution)/shard_map/ppermute | solution.py:20
  12.0 14.9 %collective-permute-start.4 = (bf16[4,6,6,512]{3,0,2,1:T(4,128)(2,1)S(1)}, bf16[4,6,6,512]{3,0,2,1:T(4,128)(2,1)S(1)}, u32[]{:S(2)}, u32[]{:S(2)}) collective-permute-start(bf16[4,6,6,512]{3,0,2,1:T(4,128)(2,1)S(1)} %get-tuple-element.21), channel_id=1, source_target_pairs={{0,12},{4,0},{8,4},{12,8},{1,13},{5,1},{9,5},{13,9},{2,14},{6,2},{... | collective-permute-start | bytes 442376 | tf_op jit(solution)/shard_map/ppermute | solution.py:20
  19.0 9.3 %collective-permute-start.1 = (bf16[4,3,12,512]{3,0,2,1:T(4,128)(2,1)}, bf16[4,3,12,512]{3,0,2,1:T(4,128)(2,1)S(1)}, u32[]{:S(2)}, u32[]{:S(2)}) collective-permute-start(bf16[4,3,12,512]{3,0,2,1:T(4,128)(2,1)} %get-tuple-element.25), channel_id=1, source_target_pairs={{0,3},{1,0},{2,1},{3,2},{4,7},{5,4},{6,5},{7,6},{8,11},{9,8},{10,9... | collective-permute-start | bytes 442376 | tf_op jit(solution)/shard_map/ppermute | solution.py:20
  27.8 5.6 %collective-permute-start.5 = (bf16[4,3,12,512]{3,0,2,1:T(4,128)(2,1)}, bf16[4,3,12,512]{3,0,2,1:T(4,128)(2,1)}, u32[]{:S(2)}, u32[]{:S(2)}) collective-permute-start(bf16[4,3,12,512]{3,0,2,1:T(4,128)(2,1)} %get-tuple-element.19), channel_id=1, source_target_pairs={{0,3},{1,0},{2,1},{3,2},{4,7},{5,4},{6,5},{7,6},{8,11},{9,8},{10,9... | collective-permute-start | bytes 442376 | tf_op jit(solution)/shard_map/ppermute | solution.py:20
  29.6 6.5 %copy-start.15 = (bf16[16,512]{1,0:T(8,128)(2,1)S(1)}, bf16[16,512]{1,0:T(8,128)(2,1)}, u32[]{:S(2)}) copy-start(bf16[16,512]{1,0:T(8,128)(2,1)} %param.21) | copy-start | bytes 49156
  29.7 7.8 %copy-start.20 = (f32[288]{0:T(512)}, f32[288]{0:T(512)S(1)}, u32[]{:S(2)}) copy-start(f32[288]{0:T(512)S(1)} %div.49) | copy-start | bytes 3460
  29.7 6.6 %copy-start.6 = (bf16[512,512]{1,0:T(8,128)(2,1)S(1)}, bf16[512,512]{1,0:T(8,128)(2,1)}, u32[]{:S(2)}) copy-start(bf16[512,512]{1,0:T(8,128)(2,1)} %param.19) | copy-start | bytes 1572868
  30.0 7.5 %copy-start.22 = (f32[288]{0:T(512)}, f32[288]{0:T(512)S(1)}, u32[]{:S(2)}) copy-start(f32[288]{0:T(512)S(1)} %rsqrt.12) | copy-start | bytes 3460
  30.1 7.5 %copy-start.25 = (f32[512]{0:T(512)S(1)}, f32[512]{0:T(512)}, u32[]{:S(2)}) copy-start(f32[512]{0:T(512)} %param.15) | copy-start | bytes 6148
  43.9 5.6 %copy-start.14 = (pred[2,144,144]{1,2,0:T(8,128)(4,1)S(1)}, pred[2,144,144]{1,2,0:T(8,128)(4,1)}, u32[]{:S(2)}) copy-start(pred[2,144,144]{1,2,0:T(8,128)(4,1)} %broadcast_compare_fusion) | copy-start | bytes 124420
  53.9 9.8 %copy-start.28 = (f32[2,8,144]{2,1,0:T(8,128)}, f32[2,8,144]{2,1,0:T(8,128)S(1)}, u32[]{:S(2)}) copy-start(f32[2,8,144]{2,1,0:T(8,128)S(1)} %get-tuple-element.28) | copy-start | bytes 27652
  86.5 5.9 %copy-start.19 = (bf16[16,512]{1,0:T(8,128)(2,1)S(1)}, bf16[16,512]{1,0:T(8,128)(2,1)}, u32[]{:S(2)}) copy-start(bf16[16,512]{1,0:T(8,128)(2,1)} %param.17) | copy-start | bytes 49156
  86.5 6.1 %copy-start.21 = (f32[288]{0:T(512)S(1)}, f32[288]{0:T(512)}, u32[]{:S(2)}) copy-start(f32[288]{0:T(512)} %copy-done.20) | copy-start | bytes 3460
  86.5 6.2 %copy-start.23 = (f32[288]{0:T(512)S(1)}, f32[288]{0:T(512)}, u32[]{:S(2)}) copy-start(f32[288]{0:T(512)} %copy-done.22) | copy-start | bytes 3460
  86.5 6.2 %copy-start.26 = (f32[512]{0:T(512)S(1)}, f32[512]{0:T(512)}, u32[]{:S(2)}) copy-start(f32[512]{0:T(512)} %param.15) | copy-start | bytes 6148
  94.9 184.8 %collective-permute-start.2 = (bf16[4,6,6,512]{3,0,2,1:T(4,128)(2,1)S(1)}, bf16[4,6,6,512]{3,0,2,1:T(4,128)(2,1)S(1)}, u32[]{:S(2)}, u32[]{:S(2)}) collective-permute-start(bf16[4,6,6,512]{3,0,2,1:T(4,128)(2,1)S(1)} %fusion.67), channel_id=1, source_target_pairs={{0,4},{4,8},{8,12},{12,0},{1,5},{5,9},{9,13},{13,1},{2,6},{6,10},{... | collective-permute-start | bytes 442376 | tf_op jit(solution)/shard_map/ppermute | solution.py:20
  95.3 181.5 %all-reduce.4.cloned.1.call-start = ((), (), s32[]{:S(2)}) async-start(), calls=%async_computation | async-start | bytes 196608 | tf_op jit(solution)/shard_map/psum | solution.py:283
  95.5 186.1 %collective-permute-start.6 = (bf16[4,6,6,512]{3,0,2,1:T(4,128)(2,1)S(1)}, bf16[4,6,6,512]{3,0,2,1:T(4,128)(2,1)S(1)}, u32[]{:S(2)}, u32[]{:S(2)}) collective-permute-start(bf16[4,6,6,512]{3,0,2,1:T(4,128)(2,1)S(1)} %fusion.65), channel_id=1, source_target_pairs={{0,4},{4,8},{8,12},{12,0},{1,5},{5,9},{9,13},{13,1},{2,6},{6,10},{... | collective-permute-start | bytes 442376 | tf_op jit(solution)/shard_map/ppermute | solution.py:20
  185.0 97.5 %copy-start.24 = (f32[16,512]{1,0:T(8,128)S(1)}, f32[16,512]{1,0:T(8,128)}, u32[]{:S(2)}) copy-start(f32[16,512]{1,0:T(8,128)} %get-tuple-element.10) | copy-start | bytes 98308
  280.0 8.2 %collective-permute-start.3 = (bf16[4,3,12,512]{3,0,2,1:T(4,128)(2,1)S(1)}, bf16[4,3,12,512]{3,0,2,1:T(4,128)(2,1)S(1)}, u32[]{:S(2)}, u32[]{:S(2)}) collective-permute-start(bf16[4,3,12,512]{3,0,2,1:T(4,128)(2,1)S(1)} %get-tuple-element.22), channel_id=1, source_target_pairs={{0,1},{1,2},{2,3},{3,0},{4,5},{5,6},{6,7},{7,4},{8,9},{9,10},{10,1... | collective-permute-start | bytes 442376 | tf_op jit(solution)/shard_map/ppermute | solution.py:20
  281.9 8.0 %collective-permute-start.7 = (bf16[4,3,12,512]{3,0,2,1:T(4,128)(2,1)S(1)}, bf16[4,3,12,512]{3,0,2,1:T(4,128)(2,1)S(1)}, u32[]{:S(2)}, u32[]{:S(2)}) collective-permute-start(bf16[4,3,12,512]{3,0,2,1:T(4,128)(2,1)S(1)} %get-tuple-element.16), channel_id=1, source_target_pairs={{0,1},{1,2},{2,3},{3,0},{4,5},{5,6},{6,7},{7,4},{8,9},{9,10},{10,1... | collective-permute-start | bytes 442376 | tf_op jit(solution)/shard_map/ppermute | solution.py:20
  (17 other events, 46.2 us)
Sparse Core Ops, SparseCore 0:
  95.4 89.6 all-reduce.5
  189.0 87.6 all-reduce.3
where the time goes:
time: 299 us; the launch traced here: 298 us
  waiting for transfers between devices  188 us (63%)
  matrix products  36.1 us (12%)
  local copies, waits for them, and re-layouts  31.5 us (11%)
  other arithmetic  16.7 us (6%)
  between operations  14.7 us (5%)
  starting transfers between devices  10.2 us (3%)
    psum x2, waiting for transfers between devices, on_device(): lax.psum((qkv_down_raw, qkv_up_raw), ('lon', 'lat'))  179 us
    ppermute x8, starting transfers between devices, from_behind(): lax.ppermute(array, axis, [(i, (i + by) % length) for i in range(length)])  10.2 us
    ppermute x8, waiting for transfers between devices, from_behind(): lax.ppermute(array, axis, [(i, (i + by) % length) for i in range(length)])  9.14 us
    unnamed x62, local copies, waits for them, and re-layouts  6.64 us
  transfers between devices with their start and end apart: 10, of which 5 were waited for; matrix products, arithmetic and copies ran while one was open for 7% of the time, Pallas kernels for 0%

commit v1 on v0

v1 whole, which is shorter than its diff:
```python
import functools
import math

import jax
import jax.numpy as jnp
import numpy as np
from jax import lax
from jax.experimental import pallas as pl
from jax.experimental.pallas import tpu as pltpu
from jax.sharding import PartitionSpec as P

HEADS = 8
WIN_LEV = 2
WIN_LAT = 6
WIN_LON = 12
REGIONS = 2
PLACES = WIN_LEV + WIN_LAT + WIN_LON

epsilon = 1e-05
barred = -1e30
MESH = pl.DeviceIdType.MESH
f32 = jnp.float32
bf16 = jnp.bfloat16


def mm(a, b):
    return jnp.dot(a, b, preferred_element_type=f32)


def mm_rows(a, b):
    return lax.dot_general(a, b, (((1,), (1,)), ((), ())), preferred_element_type=f32)


def mm_cols(a, b):
    return lax.dot_general(a, b, (((0,), (0,)), ((), ())), preferred_element_type=f32)


def kernel(n_lat, n_lon, reduce_here, grad_scale, *refs):
    (xq, gq, feat, table, gain, w_qkv, qkv_down, qkv_up, w_proj, proj_down, proj_up) = refs[:11]
    (out_o, grad_o, qd_o, qu_o, pd_o, pu_o) = refs[11:17]
    (x_in, g_in, xf, gf, normed_s, qkv_s, kf_s, attn_s, da_s, dqkv_s, probs_s) = refs[17:28]
    (o_send, b_send, o_in, b_in, terms, slots, total) = refs[28:35]
    (in_send, in_recv, out_send, out_recv, rs_send, rs_recv, ag_send, ag_recv) = refs[35:]

    lat, lon = lax.axis_index("lat"), lax.axis_index("lon")
    n = n_lat * n_lon
    me = lat * n_lon + lon

    def near(dlat, dlon):
        return {
            "lat": lax.rem(lat + dlat + n_lat, n_lat),
            "lon": lax.rem(lon + dlon + n_lon, n_lon),
        }

    def far(step):
        other = lax.rem(me + step, n)
        return other, {"lat": other // n_lon, "lon": lax.rem(other, n_lon)}

    barrier = pltpu.get_barrier_semaphore()
    if reduce_here:
        for step in range(1, n):
            pl.semaphore_signal(barrier, inc=1, device_id=far(step)[1], device_id_type=MESH)
        pl.semaphore_wait(barrier, n - 1)
    else:
        for dlat, dlon in ((0, 1), (1, 0), (1, 1)):
            for sign in (1, -1):
                pl.semaphore_signal(
                    barrier, inc=1, device_id=near(sign * dlat, sign * dlon), device_id_type=MESH
                )
        pl.semaphore_wait(barrier, 6)

    moves = []
    for kind, (src, dst) in enumerate(((xq, x_in), (gq, g_in))):
        row = []
        for quarter in (0, 1, 2):
            copy = pltpu.make_async_remote_copy(
                src_ref=src.at[quarter],
                dst_ref=dst.at[quarter],
                send_sem=in_send.at[kind, quarter],
                recv_sem=in_recv.at[kind, quarter],
                device_id=near(-1 if quarter // 2 == 0 else 0, -1 if quarter % 2 == 0 else 0),
                device_id_type=MESH,
            )
            copy.start()
            row.append(copy)
        moves.append(row)

    part = xq.shape[1]
    rows = 4 * part
    width = xq.shape[2]
    pairs = HEADS // 2
    score_scale = 1.0 / math.sqrt(width // HEADS)

    kf_s[...] = mm(feat[...], table[...]).astype(bf16)

    xf[0:part, :] = xq[3].astype(f32)
    gf[0:part, :] = gq[3].astype(f32)
    for quarter in (0, 1, 2):
        moves[0][quarter].wait()
        start = (3 - quarter) * part
        xf[start : start + part, :] = x_in[quarter].astype(f32)

    def norm():
        x = xf[...]
        centered = x - jnp.mean(x, axis=-1, keepdims=True)
        variance = jnp.mean(centered * centered, axis=-1, keepdims=True)
        inv_std = lax.rsqrt(variance + epsilon)
        return centered * inv_std, inv_std

    normed = (norm()[0] * gain[...]).astype(bf16)
    normed_s[...] = normed
    low_qkv = mm_rows(normed, qkv_down[...]).astype(bf16)
    qkv_s[...] = (mm(normed, w_qkv[...]) + mm(low_qkv, qkv_up[...])).astype(bf16)

    left = lax.broadcasted_iota(jnp.int32, (rows, 128), 1) < 64

    def pick(a, b):
        return jnp.where(left, a, b)

    def lanes(first, pair):
        return pl.ds(first + pair * 128, 128)

    def forward_pair(pair):
        query = (qkv_s[:, lanes(0, pair)].astype(f32) * score_scale)
        keys = qkv_s[:, lanes(width, pair)].astype(f32)
        values = qkv_s[:, lanes(2 * width, pair)]
        spots = feat[...].astype(f32)
        offsets = kf_s[:, lanes(0, pair)].astype(f32)
        results = []
        for half in range(2):
            if half == 0:
                q_aug, k_aug = pick(query, spots), pick(keys, offsets)
            else:
                q_aug, k_aug = pick(spots, query), pick(offsets, keys)
            scores = mm_rows(q_aug.astype(bf16), k_aug.astype(bf16))
            terms_e = jnp.exp(scores - jnp.max(scores, axis=-1, keepdims=True))
            probs = terms_e / jnp.sum(terms_e, axis=-1, keepdims=True)
            probs_s[2 * pair + half] = probs
            results.append(mm(probs.astype(bf16), values))
        attn_s[:, lanes(0, pair)] = pick(results[0], results[1]).astype(bf16)

    for pair in range(pairs):
        forward_pair(pair)

    attn = attn_s[...]
    low_proj = mm_rows(attn, proj_down[...]).astype(bf16)
    out_rows = xf[...] + mm(attn, w_proj[...]) + mm(low_proj, proj_up[...])
    for region in range(4):
        slab = out_rows[region * part : (region + 1) * part].astype(bf16)
        if region == 0:
            out_o[3] = slab
        else:
            o_send[3 - region] = slab

    def send_out(kind, src, dst):
        row = []
        for quarter in (0, 1, 2):
            copy = pltpu.make_async_remote_copy(
                src_ref=src.at[quarter],
                dst_ref=dst.at[quarter],
                send_sem=out_send.at[kind, quarter],
                recv_sem=out_recv.at[kind, quarter],
                device_id=near(1 if quarter // 2 == 0 else 0, 1 if quarter % 2 == 0 else 0),
                device_id_type=MESH,
            )
            copy.start()
            row.append(copy)
        return row

    out_moves = send_out(0, o_send, o_in)

    for quarter in (0, 1, 2):
        moves[1][quarter].wait()
        start = (3 - quarter) * part
        gf[start : start + part, :] = g_in[quarter].astype(f32)
    grad_rows = gf[...].astype(bf16)
    proj_up_raw = mm_cols(low_proj, grad_rows)
    d_low_proj = mm_rows(grad_rows, proj_up[...]).astype(bf16)
    proj_down_raw = mm_cols(d_low_proj, attn)
    da_s[...] = (mm_rows(grad_rows, w_proj[...]) + mm(d_low_proj, proj_down[...])).astype(bf16)

    def backward_pair(pair):
        query = qkv_s[:, lanes(0, pair)]
        keys = qkv_s[:, lanes(width, pair)]
        values = qkv_s[:, lanes(2 * width, pair)]
        d_attn = da_s[:, lanes(0, pair)]
        d_attn32 = d_attn.astype(f32)
        d_q, d_k, d_v = [], [], []
        for half in range(2):
            own = pick(d_attn32, 0.0) if half == 0 else pick(0.0, d_attn32)
            probs = probs_s[2 * pair + half]
            d_probs = mm_rows(own.astype(bf16), values)
            inner = jnp.sum(d_probs * probs, axis=-1, keepdims=True)
            d_scores = (probs * (d_probs - inner) * score_scale).astype(bf16)
            d_v.append(mm_cols(probs.astype(bf16), d_attn))
            d_q.append(mm(d_scores, keys))
            d_k.append(mm_cols(d_scores, query))
        dqkv_s[:, lanes(0, pair)] = pick(d_q[0], d_q[1]).astype(bf16)
        dqkv_s[:, lanes(width, pair)] = pick(d_k[0], d_k[1]).astype(bf16)
        dqkv_s[:, lanes(2 * width, pair)] = pick(d_v[0], d_v[1]).astype(bf16)

    for pair in range(pairs):
        backward_pair(pair)

    d_qkv = dqkv_s[...]
    qkv_up_raw = mm_cols(low_qkv, d_qkv)
    d_low_qkv = mm_rows(d_qkv, qkv_up[...]).astype(bf16)
    qkv_down_raw = mm_cols(d_low_qkv, normed_s[...])

    raws = ((qkv_down_raw, qd_o), (qkv_up_raw, qu_o), (proj_down_raw, pd_o), (proj_up_raw, pu_o))
    own_blocks = 0
    places = []
    if reduce_here:
        for raw, out in raws:
            for top in range(0, raw.shape[0], 8):
                for start in range(0, raw.shape[1], 128):
                    terms[len(places)] = raw[top : top + 8, start : start + 128]
                    places.append((out, top, start))
        own_blocks = len(places) // n
        scatter = []
        for step in range(1, n):
            other, where = far(step)
            copy = pltpu.make_async_remote_copy(
                src_ref=terms.at[pl.ds(other * own_blocks, own_blocks)],
                dst_ref=slots.at[step - 1],
                send_sem=rs_send.at[step - 1],
                recv_sem=rs_recv.at[step - 1],
                device_id=where,
                device_id_type=MESH,
            )
            copy.start()
            scatter.append(copy)
    else:
        for raw, out in raws:
            out[...] = raw * grad_scale

    d_normed = mm_rows(d_qkv, w_qkv[...]) + mm(d_low_qkv, qkv_down[...])
    d_unit = d_normed * gain[...]
    unit_rows, inv_std = norm()
    back = inv_std * (
        d_unit
        - jnp.mean(d_unit, axis=-1, keepdims=True)
        - unit_rows * jnp.mean(d_unit * unit_rows, axis=-1, keepdims=True)
    )
    grad_in = gf[...] + back
    for region in range(4):
        slab = grad_in[region * part : (region + 1) * part].astype(bf16)
        if region == 0:
            grad_o[3] = slab
        else:
            b_send[3 - region] = slab
    back_moves = send_out(1, b_send, b_in)

    if reduce_here:
        for copy in scatter:
            copy.wait()
        mine = pl.ds(me * own_blocks, own_blocks)
        acc = terms[mine]
        for step in range(1, n):
            acc = acc + slots[step - 1]
        total[mine] = acc * grad_scale
        gather = []
        for step in range(1, n):
            copy = pltpu.make_async_remote_copy(
                src_ref=total.at[mine],
                dst_ref=total.at[mine],
                send_sem=ag_send.at[step - 1],
                recv_sem=ag_recv.at[step - 1],
                device_id=far(step)[1],
                device_id_type=MESH,
            )
            copy.start()
            gather.append(copy)

    for quarter in (0, 1, 2):
        out_moves[quarter].wait()
        out_o[quarter] = o_in[quarter]
    for quarter in (0, 1, 2):
        back_moves[quarter].wait()
        grad_o[quarter] = b_in[quarter]

    if reduce_here:
        for step, copy in enumerate(gather, 1):
            copy.wait()
        for place, (out, top, start) in enumerate(places):
            out[top : top + 8, start : start + 128] = total[place]


def to_quarters(grid):
    levels, lat_rows, lon_cols = grid.shape[:3]
    rest = grid.shape[3:]
    blocks = grid.reshape((levels, 2, lat_rows // 2, 2, lon_cols // 2) + rest)
    order = (1, 3, 0, 2, 4) + tuple(range(5, 5 + len(rest)))
    return blocks.transpose(order).reshape((4, levels * lat_rows * lon_cols // 4) + rest)


def from_quarters(quarters, levels, lat_rows, lon_cols):
    width = quarters.shape[-1]
    blocks = quarters.reshape(2, 2, levels, lat_rows // 2, lon_cols // 2, width)
    return blocks.transpose(2, 0, 3, 1, 4, 5).reshape(levels, lat_rows, lon_cols, width)


def position_features(mask_ids):
    levels, lat_rows, lon_cols = mask_ids.shape
    grid = np.indices((2, 2, levels, lat_rows // 2, lon_cols // 2)).reshape(5, -1)
    turned = (grid[2] - WIN_LEV // 2) % levels
    lat_pos = grid[0] * (lat_rows // 2) + grid[3]
    lon_pos = grid[1] * (lon_cols // 2) + grid[4]
    spots = np.zeros((grid.shape[1], PLACES), np.float32)
    each = np.arange(grid.shape[1])
    spots[each, turned % WIN_LEV] = 1
    spots[each, WIN_LEV + lat_pos] = 1
    spots[each, WIN_LEV + WIN_LAT + lon_pos] = 1
    groups = levels // WIN_LEV * REGIONS
    ids = to_quarters(jnp.roll(mask_ids, WIN_LEV // 2, axis=0)).reshape(-1)
    ids = ids + jnp.asarray(turned // WIN_LEV * REGIONS, jnp.int32)
    group = (ids[:, None] == jnp.arange(groups, dtype=jnp.int32)).astype(bf16)
    spots = jnp.asarray(spots, bf16)
    once = jnp.concatenate((spots, spots, spots, group), 1)
    return jnp.concatenate((once, once), 1), groups


def offset_table(position_bias, groups):
    heads, columns = position_bias.shape
    place = np.arange(PLACES)
    axis = np.where(place < WIN_LEV, 0, np.where(place < WIN_LEV + WIN_LAT, 1, 2))
    first = np.array([0, WIN_LEV, WIN_LEV + WIN_LAT])[axis]
    pos = place - first
    zero = np.array(
        [WIN_LEV - 1, 2 * WIN_LEV - 1 + WIN_LAT - 1, 2 * WIN_LEV + 2 * WIN_LAT - 2 + WIN_LON - 1]
    )[axis]
    col = zero[:, None] + pos[None, :] - pos[:, None]
    same = axis[:, None] == axis[None, :]
    hot = (np.arange(columns)[:, None, None] == col[None]) & same[None]
    hot = jnp.asarray(hot.reshape(columns, PLACES * PLACES), bf16)
    high = lax.reduce_precision(position_bias, 8, 7)
    rest = position_bias - high
    middle = lax.reduce_precision(rest, 8, 7)
    low = rest - middle
    parts = jnp.stack((high, middle, low)).astype(bf16).reshape(3 * heads, columns)
    picked = mm(parts, hot).astype(bf16).reshape(3, heads, PLACES, PLACES)
    picked = picked.transpose(2, 1, 0, 3).reshape(PLACES, heads, 3 * PLACES)
    picked = jnp.pad(picked, ((0, 0), (0, 0), (0, groups)))
    walls = np.zeros((groups, heads, 3 * PLACES + groups), np.float32)
    walls[:, :, 3 * PLACES :] = (barred * (1 - np.eye(groups)))[:, None, :]
    depth = 3 * PLACES + groups
    full = jnp.concatenate(
        (
            picked,
            jnp.zeros((2 * PLACES, heads, depth), bf16),
            jnp.asarray(walls, bf16),
            jnp.zeros((depth, heads, depth), bf16),
        ),
        0,
    )
    full = full.reshape(2 * depth, heads // 2, 2, depth)[:, :, ::-1]
    return full.reshape(2 * depth, heads * depth)


def on_device(
    n_lat,
    n_lon,
    latent,
    cotangent,
    mask_ids,
    position_bias,
    norm_gain,
    w_qkv,
    qkv_down,
    qkv_up,
    w_proj,
    proj_down,
    proj_up,
):
    levels, lat_rows, lon_cols, width = latent.shape
    assert lat_rows == WIN_LAT and lon_cols == WIN_LON
    rows = levels * lat_rows * lon_cols
    part = rows // 4
    rank = qkv_down.shape[0]
    n = n_lat * n_lon
    feat, groups = position_features(mask_ids)
    table = offset_table(position_bias, groups)
    blocks = rank // 8 * (6 * width // 128)
    reduce_here = blocks % n == 0
    own = blocks // n if reduce_here else 1
    peers = n - 1 if reduce_here else 1
    grad_scale = 1.0 / math.sqrt(rows * n)
    quarter_shape = jax.ShapeDtypeStruct((4, part, width), bf16)
    dma = pltpu.SemaphoreType.DMA
    results = pl.pallas_call(
        functools.partial(kernel, n_lat, n_lon, reduce_here, grad_scale),
        out_shape=(
            quarter_shape,
            quarter_shape,
            jax.ShapeDtypeStruct((rank, width), f32),
            jax.ShapeDtypeStruct((rank, 3 * width), f32),
            jax.ShapeDtypeStruct((rank, width), f32),
            jax.ShapeDtypeStruct((rank, width), f32),
        ),
        in_specs=[pl.BlockSpec(memory_space=pltpu.VMEM)] * 11,
        out_specs=[pl.BlockSpec(memory_space=pltpu.VMEM)] * 6,
        scratch_shapes=[
            pltpu.VMEM((3, part, width), bf16),
            pltpu.VMEM((3, part, width), bf16),
            pltpu.VMEM((rows, width), f32),
            pltpu.VMEM((rows, width), f32),
            pltpu.VMEM((rows, width), bf16),
            pltpu.VMEM((rows, 3 * width), bf16),
            pltpu.VMEM((rows, width), bf16),
            pltpu.VMEM((rows, width), bf16),
            pltpu.VMEM((rows, width), bf16),
            pltpu.VMEM((rows, 3 * width), bf16),
            pltpu.VMEM((HEADS, rows, rows), f32),
            pltpu.VMEM((3, part, width), bf16),
            pltpu.VMEM((3, part, width), bf16),
            pltpu.VMEM((3, part, width), bf16),
            pltpu.VMEM((3, part, width), bf16),
            pltpu.VMEM((blocks, 8, 128), f32),
            pltpu.VMEM((peers, own, 8, 128), f32),
            pltpu.VMEM((blocks, 8, 128), f32),
            dma((2, 3)),
            dma((2, 3)),
            dma((2, 3)),
            dma((2, 3)),
            dma((peers,)),
            dma((peers,)),
            dma((peers,)),
            dma((peers,)),
        ],
        compiler_params=pltpu.CompilerParams(
            collective_id=0, has_side_effects=True, vmem_limit_bytes=60 * 2**20
        ),
        name="sublayer",
    )(
        to_quarters(latent),
        to_quarters(cotangent),
        feat,
        table,
        norm_gain.reshape(1, width),
        w_qkv,
        qkv_down,
        qkv_up,
        w_proj,
        proj_down,
        proj_up,
    )
    output = from_quarters(results[0], levels, lat_rows, lon_cols)
    latent_grad = from_quarters(results[1], levels, lat_rows, lon_cols)
    grads = results[2:]
    if not reduce_here:
        grads = lax.psum(tuple(grads), ("lon", "lat"))
    return (output, latent_grad, *grads)


def solution(mesh):
    return jax.shard_map(
        functools.partial(on_device, mesh.shape["lat"], mesh.shape["lon"]),
        mesh=mesh,
        in_specs=(
            P("runs", "lat", "lon", None),
            P("runs", "lat", "lon", None),
            P("runs", "lat", "lon"),
            P(),
            P(),
            P(),
            P(),
            P(),
            P(),
            P(),
            P(),
        ),
        out_specs=(
            P("runs", "lat", "lon", None),
            P("runs", "lat", "lon", None),
            P("runs", None),
            P("runs", None),
            P("runs", None),
            P("runs", None),
        ),
        check_vma=False,
    )
```

time: 299 us -> 53.3 us (0.18)
  waiting for transfers between devices: 188 us -> 0 us
  Pallas kernels: 0 us -> 37.2 us
  matrix products: 36.1 us -> 0.91 us
  local copies, waits for them, and re-layouts: 31.5 us -> 12.3 us
  other arithmetic: 16.7 us -> 1.65 us
  between operations: 14.7 us -> 0.82 us
  starting transfers between devices: 10.2 us -> 0 us
    psum x2 -> x0, waiting for transfers between devices: 179 us -> none  [on_device(): lax.psum((qkv_down_raw, qkv_up_raw), ('lon', 'lat'))]
    pallas_call x0 -> x1, Pallas kernels: none -> 37.2 us  [on_device(): pl.pallas_call(functools.partial(kernel, n_lat, n_lon, reduce_here, grad_...]
    dot_general x22 -> x1, matrix products: 31.8 us -> 0.91 us  [mm(): return jnp.dot(a, b, preferred_element_type=f32)]
    ppermute x8 -> x0, starting transfers between devices: 10.2 us -> none  [from_behind(): lax.ppermute(array, axis, [(i, (i + by) % length) for i in range(length)])]
    ppermute x8 -> x0, waiting for transfers between devices: 9.14 us -> none  [from_behind(): lax.ppermute(array, axis, [(i, (i + by) % length) for i in range(length)])]
    concatenate x11 -> x1, other arithmetic: 7.15 us -> 0.11 us  [offset_table(): jnp.concatenate((picked, jnp.zeros((2 * PLACES, heads, depth), bf16), jnp...]
    slice x17 -> x1, local copies, waits for them, and re-layouts: 6.21 us -> 0.71 us  [position_features(): ids = to_quarters(jnp.roll(mask_ids, WIN_LEV // 2, axis=0)).reshape(-1)]
    mul x4 -> x0, other arithmetic: 4.92 us -> none  [the longest x1 1.54 us: on_device(): qkv_up_raw * grad_scale]
  transfers between devices with their start and end apart: 10 -> 0, of which waited for: 5 -> 0; matrix products, arithmetic and copies ran while one was open for 7% -> 0% of each run, Pallas kernels for 0% -> 0%
where the time goes in v1:
time: 53.3 us; the launch traced here: 52.9 us
  Pallas kernels  37.2 us (70%)
  local copies, waits for them, and re-layouts  12.3 us (23%)
  other arithmetic  1.65 us (3%)
  matrix products  0.91 us (2%)
  between operations  0.82 us (2%)
    pallas_call x1, Pallas kernels, on_device(): pl.pallas_call(functools.partial(kernel, n_lat, n_lon, reduce_here, grad_...  37.2 us
    unnamed x22, local copies, waits for them, and re-layouts  2.84 us
    concatenate x1, local copies, waits for them, and re-layouts, position_features(): return (jnp.concatenate((once, once), 1), groups)  1.97 us
    reshape x4, local copies, waits for them, and re-layouts, to_quarters(): blocks.transpose(order)  1.76 us
    transpose x2, local copies, waits for them, and re-layouts, from_quarters(): blocks.transpose(2, 0, 3, 1, 4, 5)  1.73 us
    pallas_call x2, local copies, waits for them, and re-layouts, on_device(): pl.pallas_call(functools.partial(kernel, n_lat, n_lon, reduce_here, grad_...  1.31 us

profile of v1, /device:TPU:0, one launch (start us, length us, event | category | flops | bytes accessed | tf_op | source)
XLA Modules:
  0.0 52.9 jit_solution(4509344246201100541)
XLA Ops:
  0.8 0.7 %slice.8 = s32[1,6,12]{2,0,1:T(1,128)S(1)} slice(s32[4,6,12]{2,0,1:T(4,128)} %param.17), slice={[3:4], [0:6], [0:12]} | slice | bytes 576 | tf_op jit(solution)/shard_map/jit(_roll_static)/slice | solution.py:315
  1.5 0.7 %fusion.11 = (bf16[1,8,37]{2,1,0:T(8,128)(2,1)S(1)}, bf16[1,8,37]{2,1,0:T(8,128)(2,1)S(1)}, bf16[1,8,37]{2,1,0:T(8,128)(2,1)S(1)}) fusion(f32[8,37]{1,0:T(8,128)} %param.18), kind=kLoop, calls=%fused_computation.23 | loop fusion | flops 2072 | bytes 2960 | tf_op jit(solution)/shard_map/stack | solution.py:340
  2.2 0.7 %add_add_fusion = s32[4,6,12]{2,0,1:T(4,128)S(1)} fusion(s32[4,6,12]{2,0,1:T(4,128)} %constant.24, s32[3,6,12]{2,0,1:T(4,128)} %bitcast.54, s32[1,6,12]{2,0,1:T(1,128)S(1)} %slice.8), kind=kLoop, calls=%fused_computation.11 | loop fusion | flops 576 | bytes 3456 | tf_op jit(solution)/shard_map/add | solution.py:316
  3.1 0.1 reshape.73
  3.2 0.9 %convolution_convert_fusion = bf16[24,400]{1,0:T(8,128)(2,1)S(1)} fusion(bf16[37,400]{1,0:T(8,128)(2,1)} %constant.15.clone, bf16[1,8,37]{2,1,0:T(8,128)(2,1)S(1)} %get-tuple-element.19, bf16[1,8,37]{2,1,0:T(8,128)(2,1)S(1)} %get-tuple-element.20, bf16[1,8,37]{2,1,0:T(8,128)(2,1)S(1)} %get-tuple-element.18), kind=kOutput, calls=%fused_computation | convolution fusion | flops 721776 | bytes 50576 | tf_op jit(solution)/shard_map/dot_general | solution.py:27
  4.2 2.0 %concatenate.13.refs_2_ = bf16[288,128]{1,0:T(8,128)(2,1)} concatenate(bf16[288,20]{1,0:T(8,128)(2,1)} %constant.14.clone, bf16[288,20]{1,0:T(8,128)(2,1)} %constant.14.clone, bf16[288,20]{1,0:T(8,128)(2,1)} %constant.14.clone, bf16[288,4]{1,0:T(8,128)(2,1)S(1)} %fusion.1, bf16[288,20]{1,0:T(8,128)(2,1)} %constant.14.clone, bf16[288,20]{1,0:T(8,128)(2,1)} %constant.14.clone, ...), dimensions={1} | concatenate | bytes 147456 | tf_op jit(solution)/shard_map/concatenate | solution.py:320
  6.2 0.2 reshape.63
  6.4 0.3 copy.48
  6.7 0.1 fusion.4
  6.9 0.8 %copy.42.refs_3_ = bf16[128,512]{1,0:T(8,128)(2,1)} copy(bf16[128,512]{0,1:T(8,128)(2,1)S(1)} %bitcast.48) | data formatting | bytes 262144 | tf_op jit(solution)/shard_map/reshape | solution.py:357
  7.6 0.2 copy.54
  8.0 0.8 %copy.40.refs_0_ = bf16[4,72,512]{2,1,0:T(8,128)(2,1)} copy(bf16[4,72,512]{2,0,1:T(4,128)(2,1)S(1)} %reshape.59) | data formatting | bytes 589824 | tf_op jit(solution)/shard_map/reshape | solution.py:294
  8.7 0.2 copy.53
  9.1 0.8 %copy.41.refs_1_ = bf16[4,72,512]{2,1,0:T(8,128)(2,1)} copy(bf16[4,72,512]{2,0,1:T(4,128)(2,1)S(1)} %reshape.61) | data formatting | bytes 589824 | tf_op jit(solution)/shard_map/reshape | solution.py:294
  9.9 37.2 %sublayer.1 = (bf16[4,72,512]{2,1,0:T(8,128)(2,1)}, bf16[4,72,512]{2,1,0:T(8,128)(2,1)}, f32[16,512]{1,0:T(8,128)}, f32[16,1536]{1,0:T(8,128)}, f32[16,512]{1,0:T(8,128)}, /*index=5*/f32[16,512]{1,0:T(8,128)}) custom-call(bf16[4,72,512]{2,1,0:T(8,128)(2,1)} %copy.40.refs_0_, bf16[4,72,512]{2,1,0:T(8,128)(2,1)} %copy.41.refs_1_, ...), custom_call_target="tpu_custom_call" | custom-call | tf_op jit(solution)/shard_map/sublayer/pallas_call | solution.py:390
  47.0 1.2 %copy.43 = bf16[4,72,512]{2,0,1:T(4,128)(2,1)S(1)} copy(bf16[4,72,512]{2,1,0:T(8,128)(2,1)} %get-tuple-element.12) | data formatting | bytes 589824 | tf_op jit(solution)/shard_map/sublayer/pallas_call | solution.py:390
  48.2 0.1 reshape.68
  48.4 0.9 %copy.44 = bf16[4,2,3,2,6,512]{5,0,4,3,2,1:T(4,128)(2,1)} copy(bf16[4,2,3,2,6,512]{5,3,1,4,2,0:T(2,128)(2,1)S(1)} %bitcast.42) | data formatting | bytes 589824 | tf_op jit(solution)/shard_map/transpose | solution.py:300
  49.2 0.2 copy.45
  49.5 0.9 %copy.46 = bf16[4,2,3,2,6,512]{5,0,4,3,2,1:T(4,128)(2,1)} copy(bf16[4,2,3,2,6,512]{5,3,1,4,2,0:T(2,128)(2,1)S(1)} %bitcast.43) | data formatting | bytes 589824 | tf_op jit(solution)/shard_map/transpose | solution.py:300
  50.4 0.6 %copy.60 = f32[16,512]{1,0:T(8,128)} copy(f32[16,512]{1,0:T(8,128)S(1)} %copy-done.7) | data formatting | bytes 65536
  51.0 0.6 %copy.61 = f32[16,1536]{1,0:T(8,128)} copy(f32[16,1536]{1,0:T(8,128)S(1)} %copy-done.4) | data formatting | bytes 196608
  51.6 0.6 %copy.62 = f32[16,512]{1,0:T(8,128)} copy(f32[16,512]{1,0:T(8,128)S(1)} %copy-done.6) | data formatting | bytes 65536
  52.3 0.6 %copy.63 = f32[16,512]{1,0:T(8,128)} copy(f32[16,512]{1,0:T(8,128)S(1)} %copy-done.5) | data formatting | bytes 65536
  (28 shorter events, 0.8 us)
Async XLA Ops:
  0.6 6.1 %copy-start.3 = (bf16[4,8,64]{0,2,1:T(8,128)(2,1)S(1)}, bf16[4,8,64]{0,2,1:T(8,128)(2,1)}, u32[]{:S(2)}) copy-start(bf16[4,8,64]{0,2,1:T(8,128)(2,1)} %constant.16.clone) | copy-start | bytes 12292
  0.6 7.0 %copy-start = (bf16[4,6,12,512]{3,0,2,1:T(4,128)(2,1)S(1)}, bf16[4,6,12,512]{3,0,2,1:T(4,128)(2,1)}, u32[]{:S(2)}) copy-start(bf16[4,6,12,512]{3,0,2,1:T(4,128)(2,1)} %param.15) | copy-start | bytes 884740
  6.4 2.4 %copy-start.1 = (bf16[4,6,12,512]{3,0,2,1:T(4,128)(2,1)S(1)}, bf16[4,6,12,512]{3,0,2,1:T(4,128)(2,1)}, u32[]{:S(2)}) copy-start(bf16[4,6,12,512]{3,0,2,1:T(4,128)(2,1)} %param.16) | copy-start | bytes 884740
  47.0 2.2 %copy-start.2 = (bf16[4,72,512]{2,1,0:T(8,128)(2,1)S(1)}, bf16[4,72,512]{2,1,0:T(8,128)(2,1)}, u32[]{:S(2)}) copy-start(bf16[4,72,512]{2,1,0:T(8,128)(2,1)} %get-tuple-element.13) | copy-start | bytes 884740
  48.2 2.2 %copy-start.7 = (f32[16,512]{1,0:T(8,128)S(1)}, f32[16,512]{1,0:T(8,128)}, u32[]{:S(2)}) copy-start(f32[16,512]{1,0:T(8,128)} %get-tuple-element.29) | copy-start | bytes 98308
  48.2 2.8 %copy-start.4 = (f32[16,1536]{1,0:T(8,128)S(1)}, f32[16,1536]{1,0:T(8,128)}, u32[]{:S(2)}) copy-start(f32[16,1536]{1,0:T(8,128)} %get-tuple-element.30) | copy-start | bytes 294916
  48.2 3.4 %copy-start.6 = (f32[16,512]{1,0:T(8,128)S(1)}, f32[16,512]{1,0:T(8,128)}, u32[]{:S(2)}) copy-start(f32[16,512]{1,0:T(8,128)} %get-tuple-element.31) | copy-start | bytes 98308
  48.2 4.0 %copy-start.5 = (f32[16,512]{1,0:T(8,128)S(1)}, f32[16,512]{1,0:T(8,128)}, u32[]{:S(2)}) copy-start(f32[16,512]{1,0:T(8,128)} %get-tuple-element.32) | copy-start | bytes 98308

commit v2 on v1

--- a/solution.py
+++ b/solution.py
@@ -15,6 +15,7 @@
 WIN_LON = 12
 REGIONS = 2
 PLACES = WIN_LEV + WIN_LAT + WIN_LON
+SPOT = WIN_LEV + WIN_LAT
 
 epsilon = 1e-05
 barred = -1e30
@@ -36,11 +37,14 @@
 
 
 def kernel(n_lat, n_lon, reduce_here, grad_scale, *refs):
-    (xq, gq, feat, table, gain, w_qkv, qkv_down, qkv_up, w_proj, proj_down, proj_up) = refs[:11]
-    (out_o, grad_o, qd_o, qu_o, pd_o, pu_o) = refs[11:17]
-    (x_in, g_in, xf, gf, normed_s, qkv_s, kf_s, attn_s, da_s, dqkv_s, probs_s) = refs[17:28]
-    (o_send, b_send, o_in, b_in, terms, slots, total) = refs[28:35]
-    (in_send, in_recv, out_send, out_recv, rs_send, rs_recv, ag_send, ag_recv) = refs[35:]
+    (latent, cotangent, mask_ids, position_bias) = refs[:4]
+    (base, picker, chosen, columns, walls) = refs[4:9]
+    (gain, w_qkv, qkv_down, qkv_up, w_proj, proj_down, proj_up) = refs[9:16]
+    (out_o, grad_o, qd_o, qu_o, pd_o, pu_o) = refs[16:22]
+    (xq, gq, x_in, g_in, xf, gf, normed_s, qkv_s, kf_s, attn_s, da_s, dqkv_s, probs_s) = refs[22:35]
+    (o_send, b_send, o_in, b_in, terms, slots, total) = refs[35:42]
+    (feat, table, ids_s, grid_s, hold) = refs[42:47]
+    (in_send, in_recv, out_send, out_recv, rs_send, rs_recv, ag_send, ag_recv) = refs[47:]
 
     lat, lon = lax.axis_index("lat"), lax.axis_index("lon")
     n = n_lat * n_lon
@@ -56,18 +60,40 @@
         other = lax.rem(me + step, n)
         return other, {"lat": other // n_lon, "lon": lax.rem(other, n_lon)}
 
+    levels, lat_rows, lon_cols, width = latent.shape
+    half_rows, half_cols = lat_rows // 2, lon_cols // 2
+    part = xq.shape[1]
+    rows = 4 * part
+    pairs = HEADS // 2
+    score_scale = 1.0 / math.sqrt(width // HEADS)
+
     barrier = pltpu.get_barrier_semaphore()
     if reduce_here:
         for step in range(1, n):
             pl.semaphore_signal(barrier, inc=1, device_id=far(step)[1], device_id_type=MESH)
-        pl.semaphore_wait(barrier, n - 1)
     else:
         for dlat, dlon in ((0, 1), (1, 0), (1, 1)):
             for sign in (1, -1):
                 pl.semaphore_signal(
                     barrier, inc=1, device_id=near(sign * dlat, sign * dlon), device_id_type=MESH
                 )
-        pl.semaphore_wait(barrier, 6)
+
+    def split(grid, flat, quarters):
+        for level in range(levels):
+            for row in range(lat_rows):
+                line = grid[level, row].astype(f32)
+                for half in range(2):
+                    region = 3 - (row // half_rows * 2 + half)
+                    start = region * part + (level * half_rows + row % half_rows) * half_cols
+                    piece = line[half * half_cols : (half + 1) * half_cols]
+                    flat[start : start + half_cols, :] = piece
+        for quarter in range(3):
+            start = (3 - quarter) * part
+            quarters[quarter] = flat[start : start + part, :].astype(bf16)
+
+    split(latent, xf, xq)
+    split(cotangent, gf, gq)
+    pl.semaphore_wait(barrier, n - 1 if reduce_here else 6)
 
     moves = []
     for kind, (src, dst) in enumerate(((xq, x_in), (gq, g_in))):
@@ -85,16 +111,31 @@
             row.append(copy)
         moves.append(row)
 
-    part = xq.shape[1]
-    rows = 4 * part
-    width = xq.shape[2]
-    pairs = HEADS // 2
-    score_scale = 1.0 / math.sqrt(width // HEADS)
-
-    kf_s[...] = mm(feat[...], table[...]).astype(bf16)
-
-    xf[0:part, :] = xq[3].astype(f32)
-    gf[0:part, :] = gq[3].astype(f32)
+    ids_s[...] = jnp.zeros_like(ids_s)
+    for level in range(levels):
+        start = level * lat_rows
+        ids_s[start : start + lat_rows, SPOT : SPOT + lon_cols] = mask_ids[level].astype(f32)
+    start = levels * lat_rows
+    ids_s[start : start + 1, SPOT : SPOT + lon_cols] = jnp.ones((1, lon_cols), f32)
+    spots_f = base[...].astype(f32)
+    group = jnp.sum(mm(picker[...], ids_s[...].astype(bf16)) * spots_f, axis=-1, keepdims=True)
+    lane = lax.broadcasted_iota(jnp.int32, (rows, 128), 1)
+    lane = jnp.where(lane >= 64, lane - 64, lane) - 3 * PLACES
+    feat[...] = jnp.where(lane.astype(f32) == group, 1.0, spots_f).astype(bf16)
+
+    bias = position_bias[...]
+    high = bias.astype(bf16).astype(f32)
+    middle = (bias - high).astype(bf16).astype(f32)
+    low = bias - high - middle
+    parts = jnp.concatenate((high, middle, low), 0).astype(bf16)
+    spread = mm_cols(parts, chosen[...])
+    column = lax.broadcasted_iota(jnp.int32, spread.shape, 0)
+    table[...] = walls[...].astype(f32)
+    for place in range(PLACES):
+        hit = column == columns[place : place + 1, :]
+        table[place : place + 1, :] = jnp.sum(jnp.where(hit, spread, 0.0), axis=0, keepdims=True)
+    kf_s[...] = mm(feat[...], table[...].astype(bf16)).astype(bf16)
+
     for quarter in (0, 1, 2):
         moves[0][quarter].wait()
         start = (3 - quarter) * part
@@ -148,7 +189,7 @@
     for region in range(4):
         slab = out_rows[region * part : (region + 1) * part].astype(bf16)
         if region == 0:
-            out_o[3] = slab
+            hold[0] = slab
         else:
             o_send[3 - region] = slab
 
@@ -246,7 +287,7 @@
     for region in range(4):
         slab = grad_in[region * part : (region + 1) * part].astype(bf16)
         if region == 0:
-            grad_o[3] = slab
+            hold[1] = slab
         else:
             b_send[3 - region] = slab
     back_moves = send_out(1, b_send, b_in)
@@ -272,12 +313,24 @@
             copy.start()
             gather.append(copy)
 
-    for quarter in (0, 1, 2):
-        out_moves[quarter].wait()
-        out_o[quarter] = o_in[quarter]
-    for quarter in (0, 1, 2):
-        back_moves[quarter].wait()
-        grad_o[quarter] = b_in[quarter]
+    def join(kind, moved, arrived, out):
+        for quarter in range(4):
+            if quarter < 3:
+                moved[quarter].wait()
+                slab = arrived[quarter].astype(f32)
+            else:
+                slab = hold[kind].astype(f32)
+            first_row, first_col = quarter // 2 * half_rows, quarter % 2 * half_cols
+            for line in range(levels * half_rows):
+                grid_s[
+                    line // half_rows,
+                    first_row + line % half_rows,
+                    first_col : first_col + half_cols,
+                ] = slab[line * half_cols : (line + 1) * half_cols]
+        out[...] = grid_s[...].astype(bf16)
+
+    join(0, out_moves, o_in, out_o)
+    join(1, back_moves, b_in, grad_o)
 
     if reduce_here:
         for step, copy in enumerate(gather, 1):
@@ -286,75 +339,57 @@
             out[top : top + 8, start : start + 128] = total[place]
 
 
-def to_quarters(grid):
-    levels, lat_rows, lon_cols = grid.shape[:3]
-    rest = grid.shape[3:]
-    blocks = grid.reshape((levels, 2, lat_rows // 2, 2, lon_cols // 2) + rest)
-    order = (1, 3, 0, 2, 4) + tuple(range(5, 5 + len(rest)))
-    return blocks.transpose(order).reshape((4, levels * lat_rows * lon_cols // 4) + rest)
-
-
-def from_quarters(quarters, levels, lat_rows, lon_cols):
-    width = quarters.shape[-1]
-    blocks = quarters.reshape(2, 2, levels, lat_rows // 2, lon_cols // 2, width)
-    return blocks.transpose(2, 0, 3, 1, 4, 5).reshape(levels, lat_rows, lon_cols, width)
-
-
-def position_features(mask_ids):
-    levels, lat_rows, lon_cols = mask_ids.shape
+def finish(*refs):
+    half = len(refs) // 2
+    for source, target in zip(refs[:half], refs[half:]):
+        target[...] = source[...]
+
+
+def place_tables(levels, lat_rows, lon_cols, columns):
     grid = np.indices((2, 2, levels, lat_rows // 2, lon_cols // 2)).reshape(5, -1)
+    rows = grid.shape[1]
+    each = np.arange(rows)
     turned = (grid[2] - WIN_LEV // 2) % levels
     lat_pos = grid[0] * (lat_rows // 2) + grid[3]
     lon_pos = grid[1] * (lon_cols // 2) + grid[4]
-    spots = np.zeros((grid.shape[1], PLACES), np.float32)
-    each = np.arange(grid.shape[1])
-    spots[each, turned % WIN_LEV] = 1
-    spots[each, WIN_LEV + lat_pos] = 1
-    spots[each, WIN_LEV + WIN_LAT + lon_pos] = 1
     groups = levels // WIN_LEV * REGIONS
-    ids = to_quarters(jnp.roll(mask_ids, WIN_LEV // 2, axis=0)).reshape(-1)
-    ids = ids + jnp.asarray(turned // WIN_LEV * REGIONS, jnp.int32)
-    group = (ids[:, None] == jnp.arange(groups, dtype=jnp.int32)).astype(bf16)
-    spots = jnp.asarray(spots, bf16)
-    once = jnp.concatenate((spots, spots, spots, group), 1)
-    return jnp.concatenate((once, once), 1), groups
-
-
-def offset_table(position_bias, groups):
-    heads, columns = position_bias.shape
+    depth = 3 * PLACES + groups
+    base = np.zeros((rows, 2 * depth), np.float32)
+    for start in range(0, 3 * PLACES, PLACES):
+        for half in (0, depth):
+            base[each, half + start + turned % WIN_LEV] = 1
+            base[each, half + start + WIN_LEV + lat_pos] = 1
+            base[each, half + start + SPOT + lon_pos] = 1
+    picker = np.zeros((rows, levels * lat_rows + 8), np.float32)
+    picker[each, turned * lat_rows + lat_pos] = 1
+    picker[each, levels * lat_rows] = turned // WIN_LEV * REGIONS
+
     place = np.arange(PLACES)
-    axis = np.where(place < WIN_LEV, 0, np.where(place < WIN_LEV + WIN_LAT, 1, 2))
-    first = np.array([0, WIN_LEV, WIN_LEV + WIN_LAT])[axis]
-    pos = place - first
+    axis = np.where(place < WIN_LEV, 0, np.where(place < SPOT, 1, 2))
+    pos = place - np.array([0, WIN_LEV, SPOT])[axis]
     zero = np.array(
         [WIN_LEV - 1, 2 * WIN_LEV - 1 + WIN_LAT - 1, 2 * WIN_LEV + 2 * WIN_LAT - 2 + WIN_LON - 1]
     )[axis]
-    col = zero[:, None] + pos[None, :] - pos[:, None]
-    same = axis[:, None] == axis[None, :]
-    hot = (np.arange(columns)[:, None, None] == col[None]) & same[None]
-    hot = jnp.asarray(hot.reshape(columns, PLACES * PLACES), bf16)
-    high = lax.reduce_precision(position_bias, 8, 7)
-    rest = position_bias - high
-    middle = lax.reduce_precision(rest, 8, 7)
-    low = rest - middle
-    parts = jnp.stack((high, middle, low)).astype(bf16).reshape(3 * heads, columns)
-    picked = mm(parts, hot).astype(bf16).reshape(3, heads, PLACES, PLACES)
-    picked = picked.transpose(2, 1, 0, 3).reshape(PLACES, heads, 3 * PLACES)
-    picked = jnp.pad(picked, ((0, 0), (0, 0), (0, groups)))
-    walls = np.zeros((groups, heads, 3 * PLACES + groups), np.float32)
-    walls[:, :, 3 * PLACES :] = (barred * (1 - np.eye(groups)))[:, None, :]
-    depth = 3 * PLACES + groups
-    full = jnp.concatenate(
-        (
-            picked,
-            jnp.zeros((2 * PLACES, heads, depth), bf16),
-            jnp.asarray(walls, bf16),
-            jnp.zeros((depth, heads, depth), bf16),
-        ),
-        0,
+    col = np.where(axis[:, None] == axis[None], zero[:, None] + pos[None] - pos[:, None], -1)
+    lane = np.arange(HEADS * depth)
+    head = (lane // depth) ^ 1
+    kind = lane % depth // PLACES
+    inside = kind < 3
+    cols = np.full((PLACES + 4, HEADS * depth), -1, np.int32)
+    cols[:PLACES, inside] = col[:, lane[inside] % depth % PLACES]
+    chosen = np.zeros((3 * HEADS, HEADS * depth), np.float32)
+    chosen[kind[inside] * HEADS + head[inside], lane[inside]] = 1
+    walls = np.zeros((2 * depth, HEADS * depth), np.float32)
+    for group in range(groups):
+        other = ~inside & (lane % depth - 3 * PLACES != group)
+        walls[3 * PLACES + group, other] = barred
+    return (
+        jnp.asarray(base, bf16),
+        jnp.asarray(picker, bf16),
+        jnp.asarray(chosen, bf16),
+        jnp.asarray(cols),
+        jnp.asarray(walls, bf16),
     )
-    full = full.reshape(2 * depth, heads // 2, 2, depth)[:, :, ::-1]
-    return full.reshape(2 * depth, heads * depth)
 
 
 def on_device(
@@ -378,28 +413,31 @@
     part = rows // 4
     rank = qkv_down.shape[0]
     n = n_lat * n_lon
-    feat, groups = position_features(mask_ids)
-    table = offset_table(position_bias, groups)
+    tables = place_tables(levels, lat_rows, lon_cols, position_bias.shape[1])
     blocks = rank // 8 * (6 * width // 128)
     reduce_here = blocks % n == 0
     own = blocks // n if reduce_here else 1
     peers = n - 1 if reduce_here else 1
     grad_scale = 1.0 / math.sqrt(rows * n)
-    quarter_shape = jax.ShapeDtypeStruct((4, part, width), bf16)
+    grid_shape = jax.ShapeDtypeStruct(latent.shape, bf16)
+    shapes = (
+        grid_shape,
+        grid_shape,
+        jax.ShapeDtypeStruct((rank, width), f32),
+        jax.ShapeDtypeStruct((rank, 3 * width), f32),
+        jax.ShapeDtypeStruct((rank, width), f32),
+        jax.ShapeDtypeStruct((rank, width), f32),
+    )
+    in_vmem = pl.BlockSpec(memory_space=pltpu.VMEM)
     dma = pltpu.SemaphoreType.DMA
     results = pl.pallas_call(
         functools.partial(kernel, n_lat, n_lon, reduce_here, grad_scale),
-        out_shape=(
-            quarter_shape,
-            quarter_shape,
-            jax.ShapeDtypeStruct((rank, width), f32),
-            jax.ShapeDtypeStruct((rank, 3 * width), f32),
-            jax.ShapeDtypeStruct((rank, width), f32),
-            jax.ShapeDtypeStruct((rank, width), f32),
-        ),
-        in_specs=[pl.BlockSpec(memory_space=pltpu.VMEM)] * 11,
-        out_specs=[pl.BlockSpec(memory_space=pltpu.VMEM)] * 6,
+        out_shape=shapes,
+        in_specs=[in_vmem] * 16,
+        out_specs=[in_vmem] * 6,
         scratch_shapes=[
+            pltpu.VMEM((3, part, width), bf16),
+            pltpu.VMEM((3, part, width), bf16),
             pltpu.VMEM((3, part, width), bf16),
             pltpu.VMEM((3, part, width), bf16),
             pltpu.VMEM((rows, width), f32),
@@ -418,6 +456,11 @@
             pltpu.VMEM((blocks, 8, 128), f32),
             pltpu.VMEM((peers, own, 8, 128), f32),
             pltpu.VMEM((blocks, 8, 128), f32),
+            pltpu.VMEM((rows, 128), bf16),
+            pltpu.VMEM((128, HEADS * 64), f32),
+            pltpu.VMEM((levels * lat_rows + 8, 128), f32),
+            pltpu.VMEM(latent.shape, f32),
+            pltpu.VMEM((2, part, width), bf16),
             dma((2, 3)),
             dma((2, 3)),
             dma((2, 3)),
@@ -432,10 +475,11 @@
         ),
         name="sublayer",
     )(
-        to_quarters(latent),
-        to_quarters(cotangent),
-        feat,
-        table,
+        latent,
+        cotangent,
+        mask_ids,
+        position_bias,
+        *tables,
         norm_gain.reshape(1, width),
         w_qkv,
         qkv_down,
@@ -444,12 +488,16 @@
         proj_down,
         proj_up,
     )
-    output = from_quarters(results[0], levels, lat_rows, lon_cols)
-    latent_grad = from_quarters(results[1], levels, lat_rows, lon_cols)
-    grads = results[2:]
     if not reduce_here:
-        grads = lax.psum(tuple(grads), ("lon", "lat"))
-    return (output, latent_grad, *grads)
+        grads = lax.psum(tuple(results[2:]), ("lon", "lat"))
+        results = (*results[:2], *grads)
+    return pl.pallas_call(
+        finish,
+        out_shape=shapes,
+        in_specs=[in_vmem] * 6,
+        out_specs=[in_vmem] * 6,
+        name="finish",
+    )(*results)
 
 
 def solution(mesh):

time: 53.3 us -> 49.3 us (0.925)
  local copies, waits for them, and re-layouts: 12.3 us -> 8.76 us
  Pallas kernels: 37.2 us -> 39.6 us
  other arithmetic: 1.65 us -> 0 us
  matrix products: 0.91 us -> 0 us
    reshape x10 -> x0, local copies, waits for them, and re-layouts: 3.36 us -> none  [the longest x4 1.76 us: to_quarters(): blocks.transpose(order)]
    pallas_call x2, local copies, waits for them, and re-layouts: 1.31 us -> 3.88 us  [on_device(): pl.pallas_call(finish, out_shape=shapes, in_specs=[in_vmem] * 6, out_spec...]
    pallas_call x0 -> x1, Pallas kernels: none -> 2.13 us  [on_device(): pl.pallas_call(finish, out_shape=shapes, in_specs=[in_vmem] * 6, out_spec...]
    concatenate x3 -> x0, local copies, waits for them, and re-layouts: 2.12 us -> none  [the longest x1 1.97 us: position_features(): return (jnp.concatenate((once, once), 1), groups)]
    unnamed x22 -> x3, local copies, waits for them, and re-layouts: 2.84 us -> 4.88 us
    transpose x2 -> x0, local copies, waits for them, and re-layouts: 1.73 us -> none  [from_quarters(): blocks.transpose(2, 0, 3, 1, 4, 5)]
    dot_general x1 -> x0, matrix products: 0.91 us -> none  [mm(): return jnp.dot(a, b, preferred_element_type=f32)]
    add x1 -> x0, other arithmetic: 0.74 us -> none  [position_features(): ids = ids + jnp.asarray(turned // WIN_LEV * REGIONS, jnp.int32)]
where the time goes in v2:
time: 49.3 us; the launch traced here: 49 us
  Pallas kernels  39.6 us (80%)
  local copies, waits for them, and re-layouts  8.76 us (18%)
  between operations  0.64 us (1%)
    pallas_call x1, Pallas kernels, on_device(): pl.pallas_call(functools.partial(kernel, n_lat, n_lon, reduce_here, grad_...  37.5 us
    unnamed x3, local copies, waits for them, and re-layouts  4.88 us
    pallas_call x2, local copies, waits for them, and re-layouts, on_device(): pl.pallas_call(finish, out_shape=shapes, in_specs=[in_vmem] * 6, out_spec...  3.88 us
    pallas_call x1, Pallas kernels, on_device(): pl.pallas_call(finish, out_shape=shapes, in_specs=[in_vmem] * 6, out_spec...  2.13 us

profile of v2, /device:TPU:0, one launch (start us, length us, event | category | flops | bytes accessed | tf_op | source)
XLA Modules:
  0.0 49.0 jit_solution(14391849417592049777)
XLA Ops:
  0.6 1.3 %copy.24.refs_2_ = s32[4,6,12]{2,1,0:T(8,128)} copy(s32[4,6,12]{2,0,1:T(4,128)} %param.18) | data formatting | bytes 2304 | tf_op args[2]
  1.9 1.8 %copy.22.refs_0_ = bf16[4,6,12,512]{3,2,1,0:T(8,128)(2,1)} copy(bf16[4,6,12,512]{3,0,2,1:T(4,128)(2,1)} %param.16) | data formatting | bytes 589824 | tf_op args[0]
  3.7 1.8 %copy.23.refs_1_ = bf16[4,6,12,512]{3,2,1,0:T(8,128)(2,1)} copy(bf16[4,6,12,512]{3,0,2,1:T(4,128)(2,1)} %param.17) | data formatting | bytes 589824 | tf_op args[1]
  5.5 37.5 %sublayer.1 = (bf16[4,6,12,512]{3,2,1,0:T(8,128)(2,1)}, bf16[4,6,12,512]{3,2,1,0:T(8,128)(2,1)}, f32[16,512]{1,0:T(8,128)}, f32[16,1536]{1,0:T(8,128)}, f32[16,512]{1,0:T(8,128)}, /*index=5*/f32[16,512]{1,0:T(8,128)}) custom-call(bf16[4,6,12,512]{3,2,1,0:T(8,128)(2,1)} %copy.22.refs_0_, bf16[4,6,12,512]{3,2,1,0:T(8,128)(2,1)} %copy.23.refs_1_, ...), custom_call_target="tpu_custom_call" | custom-call | tf_op jit(solution)/shard_map/sublayer/pallas_call | solution.py:433
  43.0 2.1 %finish.1 = (bf16[4,6,12,512]{3,2,1,0:T(8,128)(2,1)}, bf16[4,6,12,512]{3,2,1,0:T(8,128)(2,1)}, f32[16,512]{1,0:T(8,128)}, f32[16,1536]{1,0:T(8,128)}, f32[16,512]{1,0:T(8,128)}, /*index=5*/f32[16,512]{1,0:T(8,128)}) custom-call(bf16[4,6,12,512]{3,2,1,0:T(8,128)(2,1)} %get-tuple-element.12.refs_0_, bf16[4,6,12,512]{3,2,1,0:T(8,128)(2,1)} %get-tuple-element.13.refs_1_, ...), custom_call_target="tpu_custom_call" | custom-call | tf_op jit(solution)/shard_map/finish/pallas_call | solution.py:494
  45.1 1.9 %copy.25 = bf16[4,6,12,512]{3,0,2,1:T(4,128)(2,1)} copy(bf16[4,6,12,512]{3,2,1,0:T(8,128)(2,1)} %get-tuple-element.18) | data formatting | bytes 589824 | tf_op jit(solution)/shard_map/finish/pallas_call | solution.py:494
  47.0 1.9 %copy.26 = bf16[4,6,12,512]{3,0,2,1:T(4,128)(2,1)} copy(bf16[4,6,12,512]{3,2,1,0:T(8,128)(2,1)} %get-tuple-element.19) | data formatting | bytes 589824 | tf_op jit(solution)/shard_map/finish/pallas_call | solution.py:494

commit v3 on v2

--- a/solution.py
+++ b/solution.py
@@ -39,12 +39,12 @@
 def kernel(n_lat, n_lon, reduce_here, grad_scale, *refs):
     (latent, cotangent, mask_ids, position_bias) = refs[:4]
     (base, picker, chosen, columns, walls) = refs[4:9]
-    (gain, w_qkv, qkv_down, qkv_up, w_proj, proj_down, proj_up) = refs[9:16]
+    (gain, w_qkv_far, qkv_down, qkv_up, w_proj_far, proj_down, proj_up) = refs[9:16]
     (out_o, grad_o, qd_o, qu_o, pd_o, pu_o) = refs[16:22]
-    (xq, gq, x_in, g_in, xf, gf, normed_s, qkv_s, kf_s, attn_s, da_s, dqkv_s, probs_s) = refs[22:35]
-    (o_send, b_send, o_in, b_in, terms, slots, total) = refs[35:42]
-    (feat, table, ids_s, grid_s, hold) = refs[42:47]
-    (in_send, in_recv, out_send, out_recv, rs_send, rs_recv, ag_send, ag_recv) = refs[47:]
+    (x_own, g_own, x_in, g_in, xf, gf, normed_s, qkv_s, kf_s, attn_s, da_s, dqkv_s, probs_s) = refs[22:35]
+    (o_send, b_send, terms, slots, total) = refs[35:40]
+    (feat, table, ids_s, w_qkv, w_proj) = refs[40:45]
+    (in_send, in_recv, out_send, out_recv, rs_send, rs_recv, ag_send, ag_recv, near_sem) = refs[45:]
 
     lat, lon = lax.axis_index("lat"), lax.axis_index("lon")
     n = n_lat * n_lon
@@ -60,9 +60,9 @@
         other = lax.rem(me + step, n)
         return other, {"lat": other // n_lon, "lon": lax.rem(other, n_lon)}
 
-    levels, lat_rows, lon_cols, width = latent.shape
+    lat_rows, lon_cols, levels, width = latent.shape
     half_rows, half_cols = lat_rows // 2, lon_cols // 2
-    part = xq.shape[1]
+    part = levels * half_rows * half_cols
     rows = 4 * part
     pairs = HEADS // 2
     score_scale = 1.0 / math.sqrt(width // HEADS)
@@ -78,29 +78,38 @@
                     barrier, inc=1, device_id=near(sign * dlat, sign * dlon), device_id_type=MESH
                 )
 
-    def split(grid, flat, quarters):
-        for level in range(levels):
-            for row in range(lat_rows):
-                line = grid[level, row].astype(f32)
-                for half in range(2):
-                    region = 3 - (row // half_rows * 2 + half)
-                    start = region * part + (level * half_rows + row % half_rows) * half_cols
-                    piece = line[half * half_cols : (half + 1) * half_cols]
-                    flat[start : start + half_cols, :] = piece
-        for quarter in range(3):
-            start = (3 - quarter) * part
-            quarters[quarter] = flat[start : start + part, :].astype(bf16)
-
-    split(latent, xf, xq)
-    split(cotangent, gf, gq)
+    def corner(grid, quarter):
+        return grid.at[
+            pl.ds(quarter // 2 * half_rows, half_rows), pl.ds(quarter % 2 * half_cols, half_cols)
+        ]
+
+    locals_ = []
+    for index, (src, dst) in enumerate(
+        (
+            (corner(latent, 3), x_own),
+            (w_qkv_far, w_qkv),
+            (corner(cotangent, 3), g_own),
+            (w_proj_far, w_proj),
+        )
+    ):
+        copy = pltpu.make_async_copy(src, dst, near_sem.at[index])
+        copy.start()
+        locals_.append(copy)
+
+    def unpack(slab, flat, region):
+        for row in range(half_rows):
+            for col in range(half_cols):
+                start = region * part + (row * half_cols + col) * levels
+                flat[start : start + levels, :] = slab[row, col].astype(f32)
+
     pl.semaphore_wait(barrier, n - 1 if reduce_here else 6)
 
     moves = []
-    for kind, (src, dst) in enumerate(((xq, x_in), (gq, g_in))):
+    for kind, (src, dst) in enumerate(((latent, x_in), (cotangent, g_in))):
         row = []
         for quarter in (0, 1, 2):
             copy = pltpu.make_async_remote_copy(
-                src_ref=src.at[quarter],
+                src_ref=corner(src, quarter),
                 dst_ref=dst.at[quarter],
                 send_sem=in_send.at[kind, quarter],
                 recv_sem=in_recv.at[kind, quarter],
@@ -112,9 +121,9 @@
         moves.append(row)
 
     ids_s[...] = jnp.zeros_like(ids_s)
-    for level in range(levels):
-        start = level * lat_rows
-        ids_s[start : start + lat_rows, SPOT : SPOT + lon_cols] = mask_ids[level].astype(f32)
+    for row in range(lat_rows):
+        start = row * levels
+        ids_s[start : start + levels, SPOT : SPOT + lon_cols] = mask_ids[row].astype(f32)
     start = levels * lat_rows
     ids_s[start : start + 1, SPOT : SPOT + lon_cols] = jnp.ones((1, lon_cols), f32)
     spots_f = base[...].astype(f32)
@@ -136,10 +145,11 @@
         table[place : place + 1, :] = jnp.sum(jnp.where(hit, spread, 0.0), axis=0, keepdims=True)
     kf_s[...] = mm(feat[...], table[...].astype(bf16)).astype(bf16)
 
+    locals_[0].wait()
+    unpack(x_own, xf, 0)
     for quarter in (0, 1, 2):
         moves[0][quarter].wait()
-        start = (3 - quarter) * part
-        xf[start : start + part, :] = x_in[quarter].astype(f32)
+        unpack(x_in.at[quarter], xf, 3 - quarter)
 
     def norm():
         x = xf[...]
@@ -151,6 +161,7 @@
     normed = (norm()[0] * gain[...]).astype(bf16)
     normed_s[...] = normed
     low_qkv = mm_rows(normed, qkv_down[...]).astype(bf16)
+    locals_[1].wait()
     qkv_s[...] = (mm(normed, w_qkv[...]) + mm(low_qkv, qkv_up[...])).astype(bf16)
 
     left = lax.broadcasted_iota(jnp.int32, (rows, 128), 1) < 64
@@ -185,20 +196,23 @@
 
     attn = attn_s[...]
     low_proj = mm_rows(attn, proj_down[...]).astype(bf16)
+    locals_[3].wait()
     out_rows = xf[...] + mm(attn, w_proj[...]) + mm(low_proj, proj_up[...])
-    for region in range(4):
-        slab = out_rows[region * part : (region + 1) * part].astype(bf16)
-        if region == 0:
-            hold[0] = slab
-        else:
-            o_send[3 - region] = slab
+    def pack(value, region, slab):
+        for row in range(half_rows):
+            for col in range(half_cols):
+                start = region * part + (row * half_cols + col) * levels
+                slab[row, col] = value[start : start + levels].astype(bf16)
+
+    for region in (3, 2, 1):
+        pack(out_rows, region, o_send.at[3 - region])
 
     def send_out(kind, src, dst):
         row = []
         for quarter in (0, 1, 2):
             copy = pltpu.make_async_remote_copy(
                 src_ref=src.at[quarter],
-                dst_ref=dst.at[quarter],
+                dst_ref=corner(dst, quarter),
                 send_sem=out_send.at[kind, quarter],
                 recv_sem=out_recv.at[kind, quarter],
                 device_id=near(1 if quarter // 2 == 0 else 0, 1 if quarter % 2 == 0 else 0),
@@ -208,12 +222,14 @@
             row.append(copy)
         return row
 
-    out_moves = send_out(0, o_send, o_in)
-
+    out_moves = send_out(0, o_send, out_o)
+    pack(out_rows, 0, corner(out_o, 3))
+
+    locals_[2].wait()
+    unpack(g_own, gf, 0)
     for quarter in (0, 1, 2):
         moves[1][quarter].wait()
-        start = (3 - quarter) * part
-        gf[start : start + part, :] = g_in[quarter].astype(f32)
+        unpack(g_in.at[quarter], gf, 3 - quarter)
     grad_rows = gf[...].astype(bf16)
     proj_up_raw = mm_cols(low_proj, grad_rows)
     d_low_proj = mm_rows(grad_rows, proj_up[...]).astype(bf16)
@@ -284,13 +300,10 @@
         - unit_rows * jnp.mean(d_unit * unit_rows, axis=-1, keepdims=True)
     )
     grad_in = gf[...] + back
-    for region in range(4):
-        slab = grad_in[region * part : (region + 1) * part].astype(bf16)
-        if region == 0:
-            hold[1] = slab
-        else:
-            b_send[3 - region] = slab
-    back_moves = send_out(1, b_send, b_in)
+    for region in (3, 2, 1):
+        pack(grad_in, region, b_send.at[3 - region])
+    back_moves = send_out(1, b_send, grad_o)
+    pack(grad_in, 0, corner(grad_o, 3))
 
     if reduce_here:
         for copy in scatter:
@@ -313,24 +326,9 @@
             copy.start()
             gather.append(copy)
 
-    def join(kind, moved, arrived, out):
-        for quarter in range(4):
-            if quarter < 3:
-                moved[quarter].wait()
-                slab = arrived[quarter].astype(f32)
-            else:
-                slab = hold[kind].astype(f32)
-            first_row, first_col = quarter // 2 * half_rows, quarter % 2 * half_cols
-            for line in range(levels * half_rows):
-                grid_s[
-                    line // half_rows,
-                    first_row + line % half_rows,
-                    first_col : first_col + half_cols,
-                ] = slab[line * half_cols : (line + 1) * half_cols]
-        out[...] = grid_s[...].astype(bf16)
-
-    join(0, out_moves, o_in, out_o)
-    join(1, back_moves, b_in, grad_o)
+    for quarter in (0, 1, 2):
+        out_moves[quarter].wait()
+        back_moves[quarter].wait()
 
     if reduce_here:
         for step, copy in enumerate(gather, 1):
@@ -346,12 +344,12 @@
 
 
 def place_tables(levels, lat_rows, lon_cols, columns):
-    grid = np.indices((2, 2, levels, lat_rows // 2, lon_cols // 2)).reshape(5, -1)
+    grid = np.indices((2, 2, lat_rows // 2, lon_cols // 2, levels)).reshape(5, -1)
     rows = grid.shape[1]
     each = np.arange(rows)
-    turned = (grid[2] - WIN_LEV // 2) % levels
-    lat_pos = grid[0] * (lat_rows // 2) + grid[3]
-    lon_pos = grid[1] * (lon_cols // 2) + grid[4]
+    turned = (grid[4] - WIN_LEV // 2) % levels
+    lat_pos = grid[0] * (lat_rows // 2) + grid[2]
+    lon_pos = grid[1] * (lon_cols // 2) + grid[3]
     groups = levels // WIN_LEV * REGIONS
     depth = 3 * PLACES + groups
     base = np.zeros((rows, 2 * depth), np.float32)
@@ -361,7 +359,7 @@
             base[each, half + start + WIN_LEV + lat_pos] = 1
             base[each, half + start + SPOT + lon_pos] = 1
     picker = np.zeros((rows, levels * lat_rows + 8), np.float32)
-    picker[each, turned * lat_rows + lat_pos] = 1
+    picker[each, lat_pos * levels + turned] = 1
     picker[each, levels * lat_rows] = turned // WIN_LEV * REGIONS
 
     place = np.arange(PLACES)
@@ -419,7 +417,9 @@
     own = blocks // n if reduce_here else 1
     peers = n - 1 if reduce_here else 1
     grad_scale = 1.0 / math.sqrt(rows * n)
-    grid_shape = jax.ShapeDtypeStruct(latent.shape, bf16)
+    grid_shape = jax.ShapeDtypeStruct((lat_rows, lon_cols, levels, width), bf16)
+    slab = (lat_rows // 2, lon_cols // 2, levels, width)
+    in_place = pl.BlockSpec(memory_space=pl.ANY)
     shapes = (
         grid_shape,
         grid_shape,
@@ -433,13 +433,15 @@
     results = pl.pallas_call(
         functools.partial(kernel, n_lat, n_lon, reduce_here, grad_scale),
         out_shape=shapes,
-        in_specs=[in_vmem] * 16,
+        in_specs=[
+            in_place if index in (0, 1, 10, 13) else in_vmem for index in range(16)
+        ],
         out_specs=[in_vmem] * 6,
         scratch_shapes=[
-            pltpu.VMEM((3, part, width), bf16),
-            pltpu.VMEM((3, part, width), bf16),
-            pltpu.VMEM((3, part, width), bf16),
-            pltpu.VMEM((3, part, width), bf16),
+            pltpu.VMEM(slab, bf16),
+            pltpu.VMEM(slab, bf16),
+            pltpu.VMEM((3, *slab), bf16),
+            pltpu.VMEM((3, *slab), bf16),
             pltpu.VMEM((rows, width), f32),
             pltpu.VMEM((rows, width), f32),
             pltpu.VMEM((rows, width), bf16),
@@ -449,18 +451,16 @@
             pltpu.VMEM((rows, width), bf16),
             pltpu.VMEM((rows, 3 * width), bf16),
             pltpu.VMEM((HEADS, rows, rows), f32),
-            pltpu.VMEM((3, part, width), bf16),
-            pltpu.VMEM((3, part, width), bf16),
-            pltpu.VMEM((3, part, width), bf16),
-            pltpu.VMEM((3, part, width), bf16),
+            pltpu.VMEM((3, *slab), bf16),
+            pltpu.VMEM((3, *slab), bf16),
             pltpu.VMEM((blocks, 8, 128), f32),
             pltpu.VMEM((peers, own, 8, 128), f32),
             pltpu.VMEM((blocks, 8, 128), f32),
             pltpu.VMEM((rows, 128), bf16),
             pltpu.VMEM((128, HEADS * 64), f32),
             pltpu.VMEM((levels * lat_rows + 8, 128), f32),
-            pltpu.VMEM(latent.shape, f32),
-            pltpu.VMEM((2, part, width), bf16),
+            pltpu.VMEM((width, 3 * width), bf16),
+            pltpu.VMEM((width, width), bf16),
             dma((2, 3)),
             dma((2, 3)),
             dma((2, 3)),
@@ -469,15 +469,16 @@
             dma((peers,)),
             dma((peers,)),
             dma((peers,)),
+            dma((4,)),
         ],
         compiler_params=pltpu.CompilerParams(
             collective_id=0, has_side_effects=True, vmem_limit_bytes=60 * 2**20
         ),
         name="sublayer",
     )(
-        latent,
-        cotangent,
-        mask_ids,
+        latent.transpose(1, 2, 0, 3),
+        cotangent.transpose(1, 2, 0, 3),
+        mask_ids.transpose(1, 0, 2),
         position_bias,
         *tables,
         norm_gain.reshape(1, width),
@@ -491,13 +492,14 @@
     if not reduce_here:
         grads = lax.psum(tuple(results[2:]), ("lon", "lat"))
         results = (*results[:2], *grads)
-    return pl.pallas_call(
+    output, latent_grad, *grads = pl.pallas_call(
         finish,
         out_shape=shapes,
         in_specs=[in_vmem] * 6,
         out_specs=[in_vmem] * 6,
         name="finish",
     )(*results)
+    return (output.transpose(2, 0, 1, 3), latent_grad.transpose(2, 0, 1, 3), *grads)
 
 
 def solution(mesh):

time: 49.3 us -> 39.9 us (0.81)
  local copies, waits for them, and re-layouts: 8.76 us -> 0 us
  Pallas kernels: 39.6 us -> 39.1 us
    unnamed x3 -> x0, local copies, waits for them, and re-layouts: 4.88 us -> none
    pallas_call x2 -> x0, local copies, waits for them, and re-layouts: 3.88 us -> none  [on_device(): pl.pallas_call(finish, out_shape=shapes, in_specs=[in_vmem] * 6, out_spec...]
where the time goes in v3:
time: 39.9 us; the launch traced here: 39.7 us
  Pallas kernels  39.1 us (98%)
  between operations  0.64 us (2%)
    pallas_call x1, Pallas kernels, on_device(): pl.pallas_call(functools.partial(kernel, n_lat, n_lon, reduce_here, grad_...  37.1 us
    pallas_call x1, Pallas kernels, on_device(): pl.pallas_call(finish, out_shape=shapes, in_specs=[in_vmem] * 6, out_spec...  1.99 us

profile of v3, /device:TPU:0, one launch (start us, length us, event | category | flops | bytes accessed | tf_op | source)
XLA Modules:
  0.0 39.7 jit_solution(12894583052532044342)
XLA Ops:
  0.6 37.1 %sublayer.1 = (bf16[6,12,4,512]{3,2,1,0:T(4,128)(2,1)}, bf16[6,12,4,512]{3,2,1,0:T(4,128)(2,1)}, f32[16,512]{1,0:T(8,128)}, f32[16,1536]{1,0:T(8,128)}, f32[16,512]{1,0:T(8,128)}, /*index=5*/f32[16,512]{1,0:T(8,128)}) custom-call(bf16[6,12,4,512]{3,2,1,0:T(4,128)(2,1)} %bitcast.6, bf16[6,12,4,512]{3,2,1,0:T(4,128)(2,1)} %bitcast.7, s32[6,4,12]{2,1,0:T(4,128)} %bitcast.8, ...), custom_call_target="tpu_custom_call" | custom-call | tf_op jit(solution)/shard_map/sublayer/pallas_call | solution.py:433
  37.7 2.0 %finish.1 = (bf16[6,12,4,512]{3,2,1,0:T(4,128)(2,1)}, bf16[6,12,4,512]{3,2,1,0:T(4,128)(2,1)}, f32[16,512]{1,0:T(8,128)}, f32[16,1536]{1,0:T(8,128)}, f32[16,512]{1,0:T(8,128)}, /*index=5*/f32[16,512]{1,0:T(8,128)}) custom-call(bf16[6,12,4,512]{3,2,1,0:T(4,128)(2,1)} %get-tuple-element.18.refs_0_, bf16[6,12,4,512]{3,2,1,0:T(4,128)(2,1)} %get-tuple-element.19.refs_1_, ...), custom_call_target="tpu_custom_call" | custom-call | tf_op jit(solution)/shard_map/finish/pallas_call | solution.py:495

commit v4 on v3

--- a/solution.py
+++ b/solution.py
@@ -271,7 +271,7 @@
         for raw, out in raws:
             for top in range(0, raw.shape[0], 8):
                 for start in range(0, raw.shape[1], 128):
-                    terms[len(places)] = raw[top : top + 8, start : start + 128]
+                    terms[len(places)] = raw[top : top + 8, start : start + 128].astype(bf16)
                     places.append((out, top, start))
         own_blocks = len(places) // n
         scatter = []
@@ -309,10 +309,10 @@
         for copy in scatter:
             copy.wait()
         mine = pl.ds(me * own_blocks, own_blocks)
-        acc = terms[mine]
+        acc = terms[mine].astype(f32)
         for step in range(1, n):
-            acc = acc + slots[step - 1]
-        total[mine] = acc * grad_scale
+            acc = acc + slots[step - 1].astype(f32)
+        total[mine] = acc.astype(bf16)
         gather = []
         for step in range(1, n):
             copy = pltpu.make_async_remote_copy(
@@ -334,7 +334,7 @@
         for step, copy in enumerate(gather, 1):
             copy.wait()
         for place, (out, top, start) in enumerate(places):
-            out[top : top + 8, start : start + 128] = total[place]
+            out[top : top + 8, start : start + 128] = total[place].astype(f32) * grad_scale
 
 
 def finish(*refs):
@@ -453,9 +453,9 @@
             pltpu.VMEM((HEADS, rows, rows), f32),
             pltpu.VMEM((3, *slab), bf16),
             pltpu.VMEM((3, *slab), bf16),
-            pltpu.VMEM((blocks, 8, 128), f32),
-            pltpu.VMEM((peers, own, 8, 128), f32),
-            pltpu.VMEM((blocks, 8, 128), f32),
+            pltpu.VMEM((blocks, 8, 128), bf16),
+            pltpu.VMEM((peers, own, 8, 128), bf16),
+            pltpu.VMEM((blocks, 8, 128), bf16),
             pltpu.VMEM((rows, 128), bf16),
             pltpu.VMEM((128, HEADS * 64), f32),
             pltpu.VMEM((levels * lat_rows + 8, 128), f32),

time: 39.9 us -> 37.1 us (0.930)
  Pallas kernels: 39.1 us -> 36.3 us
    pallas_call x1, Pallas kernels: 37.1 us -> 34.3 us  [on_device(): pl.pallas_call(functools.partial(kernel, n_lat, n_lon, reduce_here, grad_...]
where the time goes in v4:
time: 37.1 us; the launch traced here: 37 us
  Pallas kernels  36.3 us (98%)
  between operations  0.64 us (2%)
    pallas_call x1, Pallas kernels, on_device(): pl.pallas_call(functools.partial(kernel, n_lat, n_lon, reduce_here, grad_...  34.3 us
    pallas_call x1, Pallas kernels, on_device(): pl.pallas_call(finish, out_shape=shapes, in_specs=[in_vmem] * 6, out_spec...  1.99 us

profile of v4, /device:TPU:0, one launch (start us, length us, event | category | flops | bytes accessed | tf_op | source)
XLA Modules:
  0.0 37.0 jit_solution(17783542914066146359)
XLA Ops:
  0.6 34.3 %sublayer.1 = (bf16[6,12,4,512]{3,2,1,0:T(4,128)(2,1)}, bf16[6,12,4,512]{3,2,1,0:T(4,128)(2,1)}, f32[16,512]{1,0:T(8,128)}, f32[16,1536]{1,0:T(8,128)}, f32[16,512]{1,0:T(8,128)}, /*index=5*/f32[16,512]{1,0:T(8,128)}) custom-call(bf16[6,12,4,512]{3,2,1,0:T(4,128)(2,1)} %bitcast.6, bf16[6,12,4,512]{3,2,1,0:T(4,128)(2,1)} %bitcast.7, s32[6,4,12]{2,1,0:T(4,128)} %bitcast.8, ...), custom_call_target="tpu_custom_call" | custom-call | tf_op jit(solution)/shard_map/sublayer/pallas_call | solution.py:433
  35.0 2.0 %finish.1 = (bf16[6,12,4,512]{3,2,1,0:T(4,128)(2,1)}, bf16[6,12,4,512]{3,2,1,0:T(4,128)(2,1)}, f32[16,512]{1,0:T(8,128)}, f32[16,1536]{1,0:T(8,128)}, f32[16,512]{1,0:T(8,128)}, /*index=5*/f32[16,512]{1,0:T(8,128)}) custom-call(bf16[6,12,4,512]{3,2,1,0:T(4,128)(2,1)} %get-tuple-element.18.refs_0_, bf16[6,12,4,512]{3,2,1,0:T(4,128)(2,1)} %get-tuple-element.19.refs_1_, ...), custom_call_target="tpu_custom_call" | custom-call | tf_op jit(solution)/shard_map/finish/pallas_call | solution.py:495

commit v5 on v4

--- a/solution.py
+++ b/solution.py
@@ -235,6 +235,36 @@
     d_low_proj = mm_rows(grad_rows, proj_up[...]).astype(bf16)
     proj_down_raw = mm_cols(d_low_proj, attn)
     da_s[...] = (mm_rows(grad_rows, w_proj[...]) + mm(d_low_proj, proj_down[...])).astype(bf16)
+
+    own = terms.shape[1]
+    places = []
+    scatter = []
+
+    def place_terms(raws, first, count):
+        index = 0
+        for raw, out in raws:
+            for top in range(0, raw.shape[0], 8):
+                for start in range(0, raw.shape[1], 128):
+                    owner, slot = index // count, first + index % count
+                    terms[owner, slot] = raw[top : top + 8, start : start + 128].astype(bf16)
+                    places.append((owner, slot, out, top, start))
+                    index += 1
+        batch = 0 if first == 0 else 1
+        for step in range(1, n):
+            other, where = far(step)
+            copy = pltpu.make_async_remote_copy(
+                src_ref=terms.at[other, pl.ds(first, count)],
+                dst_ref=slots.at[step - 1, pl.ds(first, count)],
+                send_sem=rs_send.at[batch, step - 1],
+                recv_sem=rs_recv.at[batch, step - 1],
+                device_id=where,
+                device_id_type=MESH,
+            )
+            copy.start()
+            scatter.append(copy)
+
+    if reduce_here:
+        place_terms(((proj_down_raw, pd_o), (proj_up_raw, pu_o)), 0, own // 3)
 
     def backward_pair(pair):
         query = qkv_s[:, lanes(0, pair)]
@@ -264,31 +294,15 @@
     d_low_qkv = mm_rows(d_qkv, qkv_up[...]).astype(bf16)
     qkv_down_raw = mm_cols(d_low_qkv, normed_s[...])
 
-    raws = ((qkv_down_raw, qd_o), (qkv_up_raw, qu_o), (proj_down_raw, pd_o), (proj_up_raw, pu_o))
-    own_blocks = 0
-    places = []
     if reduce_here:
-        for raw, out in raws:
-            for top in range(0, raw.shape[0], 8):
-                for start in range(0, raw.shape[1], 128):
-                    terms[len(places)] = raw[top : top + 8, start : start + 128].astype(bf16)
-                    places.append((out, top, start))
-        own_blocks = len(places) // n
-        scatter = []
-        for step in range(1, n):
-            other, where = far(step)
-            copy = pltpu.make_async_remote_copy(
-                src_ref=terms.at[pl.ds(other * own_blocks, own_blocks)],
-                dst_ref=slots.at[step - 1],
-                send_sem=rs_send.at[step - 1],
-                recv_sem=rs_recv.at[step - 1],
-                device_id=where,
-                device_id_type=MESH,
-            )
-            copy.start()
-            scatter.append(copy)
+        place_terms(((qkv_down_raw, qd_o), (qkv_up_raw, qu_o)), own // 3, own - own // 3)
     else:
-        for raw, out in raws:
+        for raw, out in (
+            (qkv_down_raw, qd_o),
+            (qkv_up_raw, qu_o),
+            (proj_down_raw, pd_o),
+            (proj_up_raw, pu_o),
+        ):
             out[...] = raw * grad_scale
 
     d_normed = mm_rows(d_qkv, w_qkv[...]) + mm(d_low_qkv, qkv_down[...])
@@ -308,16 +322,15 @@
     if reduce_here:
         for copy in scatter:
             copy.wait()
-        mine = pl.ds(me * own_blocks, own_blocks)
-        acc = terms[mine].astype(f32)
+        acc = terms[me].astype(f32)
         for step in range(1, n):
             acc = acc + slots[step - 1].astype(f32)
-        total[mine] = acc.astype(bf16)
+        total[me] = acc.astype(bf16)
         gather = []
         for step in range(1, n):
             copy = pltpu.make_async_remote_copy(
-                src_ref=total.at[mine],
-                dst_ref=total.at[mine],
+                src_ref=total.at[me],
+                dst_ref=total.at[me],
                 send_sem=ag_send.at[step - 1],
                 recv_sem=ag_recv.at[step - 1],
                 device_id=far(step)[1],
@@ -333,8 +346,8 @@
     if reduce_here:
         for step, copy in enumerate(gather, 1):
             copy.wait()
-        for place, (out, top, start) in enumerate(places):
-            out[top : top + 8, start : start + 128] = total[place].astype(f32) * grad_scale
+        for owner, slot, out, top, start in places:
+            out[top : top + 8, start : start + 128] = total[owner, slot].astype(f32) * grad_scale
 
 
 def finish(*refs):
@@ -413,8 +426,9 @@
     n = n_lat * n_lon
     tables = place_tables(levels, lat_rows, lon_cols, position_bias.shape[1])
     blocks = rank // 8 * (6 * width // 128)
-    reduce_here = blocks % n == 0
+    reduce_here = blocks % (3 * n) == 0
     own = blocks // n if reduce_here else 1
+    owners = n if reduce_here else 1
     peers = n - 1 if reduce_here else 1
     grad_scale = 1.0 / math.sqrt(rows * n)
     grid_shape = jax.ShapeDtypeStruct((lat_rows, lon_cols, levels, width), bf16)
@@ -453,9 +467,9 @@
             pltpu.VMEM((HEADS, rows, rows), f32),
             pltpu.VMEM((3, *slab), bf16),
             pltpu.VMEM((3, *slab), bf16),
-            pltpu.VMEM((blocks, 8, 128), bf16),
+            pltpu.VMEM((owners, own, 8, 128), bf16),
             pltpu.VMEM((peers, own, 8, 128), bf16),
-            pltpu.VMEM((blocks, 8, 128), bf16),
+            pltpu.VMEM((owners, own, 8, 128), bf16),
             pltpu.VMEM((rows, 128), bf16),
             pltpu.VMEM((128, HEADS * 64), f32),
             pltpu.VMEM((levels * lat_rows + 8, 128), f32),
@@ -465,8 +479,8 @@
             dma((2, 3)),
             dma((2, 3)),
             dma((2, 3)),
-            dma((peers,)),
-            dma((peers,)),
+            dma((2, peers)),
+            dma((2, peers)),
             dma((peers,)),
             dma((peers,)),
             dma((4,)),

time: 37.1 us -> 37.2 us (level)
  no operation moved by 1% of the time
where the time goes in v5:
time: 37.2 us; the launch traced here: 37.1 us
  Pallas kernels  36.4 us (98%)
  between operations  0.64 us (2%)
    pallas_call x1, Pallas kernels, on_device(): pl.pallas_call(functools.partial(kernel, n_lat, n_lon, reduce_here, grad_...  34.4 us
    pallas_call x1, Pallas kernels, on_device(): pl.pallas_call(finish, out_shape=shapes, in_specs=[in_vmem] * 6, out_spec...  1.99 us

profile of v5, /device:TPU:0, one launch (start us, length us, event | category | flops | bytes accessed | tf_op | source)
XLA Modules:
  0.0 37.1 jit_solution(13534536178114190873)
XLA Ops:
  0.6 34.4 %sublayer.1 = (bf16[6,12,4,512]{3,2,1,0:T(4,128)(2,1)}, bf16[6,12,4,512]{3,2,1,0:T(4,128)(2,1)}, f32[16,512]{1,0:T(8,128)}, f32[16,1536]{1,0:T(8,128)}, f32[16,512]{1,0:T(8,128)}, /*index=5*/f32[16,512]{1,0:T(8,128)}) custom-call(bf16[6,12,4,512]{3,2,1,0:T(4,128)(2,1)} %bitcast.6, bf16[6,12,4,512]{3,2,1,0:T(4,128)(2,1)} %bitcast.7, s32[6,4,12]{2,1,0:T(4,128)} %bitcast.8, ...), custom_call_target="tpu_custom_call" | custom-call | tf_op jit(solution)/shard_map/sublayer/pallas_call | solution.py:447
  35.1 2.0 %finish.1 = (bf16[6,12,4,512]{3,2,1,0:T(4,128)(2,1)}, bf16[6,12,4,512]{3,2,1,0:T(4,128)(2,1)}, f32[16,512]{1,0:T(8,128)}, f32[16,1536]{1,0:T(8,128)}, f32[16,512]{1,0:T(8,128)}, /*index=5*/f32[16,512]{1,0:T(8,128)}) custom-call(bf16[6,12,4,512]{3,2,1,0:T(4,128)(2,1)} %get-tuple-element.18.refs_0_, bf16[6,12,4,512]{3,2,1,0:T(4,128)(2,1)} %get-tuple-element.19.refs_1_, ...), custom_call_target="tpu_custom_call" | custom-call | tf_op jit(solution)/shard_map/finish/pallas_call | solution.py:509
